TPU v7x, 256 devices: a whole 4x4x8 slice. The times are simulated.
256 devices in a mesh: rep: 8 (over y, core), shard: 32 (over z, x).
Axes of the slice: x: 4, y: 4, z: 8, core: 2. Of those that a mesh axis runs over, the one named last changes fastest.
Arguments:
- grad_kv: bfloat16 [8, 2, 8192, 1024], P('rep', None, 'shard'), may hold values from -24 to 24
- error_kv: float32 [8, 2, 8192, 1024], P('rep', None, 'shard'), may hold values from -12 to 12
- basis_kv: float32 [2, 1024, 64], replicated, may hold values from -6 to 6
Outputs:
- update_kv: bfloat16 [2, 8192, 1024], P(None, 'shard')
- new_error: float32 [8, 2, 8192, 1024], P('rep', None, 'shard')
- basis_next: float32 [2, 1024, 64], replicated
All inputs are finite; a program needn't handle non-finite values.
Results may differ from a plain program's by a relative error of at most 0.001.
Values sent between devices are 32-bit elements; how exact they have to be, the bound alone decides.
A program may use at most 64 MiB of HBM per device.

v0:
```python
import jax
import jax.numpy as jnp
from jax import lax
from jax.sharding import Mesh
from jax.sharding import PartitionSpec as P

REP = ("rep_0", "rep_1")
SHARD = ("shard_0", "shard_1")


def sent_to_all(x, axis):
    count = lax.axis_size(axis)
    return lax.all_to_all(jnp.broadcast_to(x[None], (count, *x.shape)), axis, 0, 0, tiled=True)


def over_copies(x, axis):
    everything = sent_to_all(x, axis)
    return jnp.sum(everything, axis=0)


def padded_to(lines, count):
    spare = -len(lines) % count
    return jnp.pad(lines, [(0, spare)] + [(0, 0)] * (lines.ndim - 1))


def joined_along(tiles, dim):
    lengths = list(tiles.shape[1:])
    lengths[dim] *= tiles.shape[0]
    return jnp.moveaxis(tiles, 0, dim).reshape(lengths)


def gather_axes(x, axes, dim):
    far, near = axes
    tiles = sent_to_all(sent_to_all(x, far), near)
    return joined_along(tiles.swapaxes(0, 1).reshape(-1, *x.shape), dim)


def cut_along(x, dim, count):
    lengths = x.shape
    tiles = x.reshape(*lengths[:dim], count, lengths[dim] // count, *lengths[dim + 1 :])
    return jnp.moveaxis(tiles, dim, 0)


def sum_at_owner(x, axis, dim):
    tiles = cut_along(x, dim, lax.axis_size(axis))
    arrived = lax.all_to_all(tiles, axis, split_axis=0, concat_axis=0, tiled=True)
    return arrived.sum(axis=0)


def sum_by_axis(x, axes, dim):
    far, near = axes
    own = sum_at_owner(cut_along(x, dim, lax.axis_size(far)), near, dim + 1)
    return jnp.sum(lax.all_to_all(own, far, 0, 0, tiled=True), axis=0)


def nested_sum(x, axes):
    padded = padded_to(x, lax.axis_size(axes[0]) * lax.axis_size(axes[1]))
    whole = gather_axes(sum_by_axis(padded, axes, 0), axes, 0)
    return lax.slice_in_dim(whole, 0, len(x)).reshape(x.shape)


def together(arrays, axis):
    vector, at, gathered = (jnp.concatenate([a.reshape(-1) for a in arrays]), 0, [])
    subtotal = nested_sum(vector, axis)
    for a in arrays:
        gathered.append(subtotal[at : at + a.size].reshape(a.shape))
        at += a.size
    return tuple(gathered)


def orthogonal(left, gram):
    chol = jnp.linalg.cholesky(gram)
    ortho = lax.linalg.triangular_solve(chol, left, left_side=False, lower=True, transpose_a=True)
    return (chol, ortho)


def on_device(grad_kv, error_kv, basis_kv):
    highest = lax.Precision.HIGHEST
    replicas = lax.axis_size(REP)
    merged = grad_kv[0].astype(jnp.float32) + error_kv[0]
    local_left = jnp.einsum("mrc,mck->mrk", merged, basis_kv, precision=highest)
    left = over_copies(local_left, REP) / replicas
    local_gram = jnp.einsum("mrk,mrl->mkl", left, left, precision=highest)
    local_right = jnp.einsum("mrc,mrk->mck", merged, left, precision=highest)
    summed, gram = together(
        (local_right, local_gram / replicas), (("rep_0", "rep_1", "shard_0"), "shard_1")
    )
    chol, ortho = orthogonal(left, gram)
    right = (
        lax.linalg.triangular_solve(chol, summed, left_side=False, lower=True, transpose_a=True)
        / replicas
    )
    approx = jnp.einsum("mrk,mck->mrc", ortho, right, precision=highest)
    new_error = (merged - approx)[None]
    return (approx.astype(jnp.bfloat16), new_error, right)


def solution(mesh):
    torus = Mesh(mesh.devices.reshape(4, 2, 8, 4), ("rep_0", "rep_1", "shard_0", "shard_1"))
    placed = (P(REP, None, SHARD, None), P(REP, None, SHARD, None), P())
    return jax.shard_map(
        on_device,
        mesh=torus,
        in_specs=placed,
        out_specs=(P(None, SHARD, None), P(REP, None, SHARD, None), P()),
        check_vma=False,
    )
```

profile of v0, /device:TPU:1, one launch (start us, length us, event | category | flops | bytes accessed | tf_op | source)
XLA Modules:
  0.0 141.6 jit_solution(15423510714517279978)
XLA Ops:
  0.6 0.0 copy-start
  0.6 1.0 copy-done
  1.7 4.1 %fusion.2 = f32[2,256,64]{1,2,0:T(8,128)S(1)} fusion(f32[2,1024,64]{1,2,0:T(8,128)S(1)} %copy-done, f32[1,2,256,1024]{3,2,1,0:T(8,128)} %param.4, bf16[1,2,256,1024]{3,2,1,0:T(8,128)(2,1)} %param.3), kind=kOutput, calls=%fused_computation.3 | convolution fusion | flops 403701760 | bytes 3801088 | tf_op jit(solution)/shard_map/mrc,mck->mrk/dot_general | solution.py:81
  5.8 0.0 copy-start.1
  5.8 0.1 broadcast_in_dim.12
  5.9 21.4 %all_to_all.30 = f32[8,2,256,64]{2,3,1,0:T(8,128)} all-to-all(f32[8,2,256,64]{2,3,1,0:T(8,128)S(1)} %broadcast_in_dim.12), channel_id=1, replica_groups=mesh['rep_0'=4,'rep_1'=2,'shard_0'=8,'shard_1'=4] {'rep_0','rep_1'}, dimensions={0} | all-to-all | bytes 2097152 | tf_op jit(solution)/shard_map/all_to_all | solution.py:13
  27.3 1.3 reduce_sum.27
  28.6 0.3 convolution_multiply_fusion.1
  28.8 0.0 copy-done.1
  28.9 5.6 %fusion = f32[2,1024,64]{2,1,0:T(8,128)} fusion(f32[1,2,256,1024]{3,2,1,0:T(8,128)S(1)} %copy-done.1, bf16[1,2,256,1024]{3,2,1,0:T(8,128)(2,1)} %param.3, f32[2,256,64]{1,2,0:T(8,128)S(1)} %reduce_sum.27), kind=kOutput, calls=%fused_computation.1 | convolution fusion | flops 403734528 | bytes 3801088 | tf_op jit(solution)/shard_map/mrc,mrk->mck/dot_general | solution.py:84
  34.5 0.1 reshape.44
  34.6 1.4 %reshape.43 = f32[131072]{0:T(1024)S(1)} reshape(f32[2,1024,64]{2,1,0:T(8,128)} %fusion) | data formatting | bytes 1048576 | tf_op jit(solution)/shard_map/reshape | solution.py:63
  36.0 0.8 pad_maximum_fusion
  36.8 1.5 %reshape_reshape.6 = f32[64,4,544]{2,1,0:T(4,128)S(1)} reshape(f32[139264]{0:T(1024)} %pad_maximum_fusion) | data formatting | bytes 1114112 | tf_op jit(solution)/shard_map/reshape;reshape | solution.py:40
  38.4 12.7 %all_to_all.31 = f32[4,64,544]{2,1,0:T(8,128)S(1)} all-to-all(f32[4,64,544]{2,1,0:T(8,128)S(1)} %copy.33), channel_id=1, replica_groups=mesh['rep_0'=4,'rep_1'=2,'shard_0'=8,'shard_1'=4] {'shard_1'}, dimensions={0} | all-to-all | bytes 1114112 | tf_op jit(solution)/shard_map/all_to_all | solution.py:46
  51.2 0.7 reduce_sum.28
  51.9 1.0 all_to_all.21
  52.9 22.2 %all_to_all.32 = f32[64,1,544]{2,1,0:T(1,128)S(1)} all-to-all(f32[64,1,544]{2,1,0:T(1,128)S(1)} %all_to_all.21), channel_id=1, replica_groups=mesh['rep_0'=4,'rep_1'=2,'shard_0'=8,'shard_1'=4] {'rep_0','rep_1','shar..., dimensions={0} | all-to-all | bytes 278528 | tf_op jit(solution)/shard_map/all_to_all | solution.py:53
  75.1 0.1 reduce_sum.29
  75.3 0.1 broadcast_in_dim.13
  75.4 15.8 %all_to_all.33 = f32[64,1,544]{2,1,0:T(1,128)S(1)} all-to-all(f32[64,1,544]{2,1,0:T(1,128)S(1)} %broadcast_in_dim.13), channel_id=1, replica_groups=mesh['rep_0'=4,'rep_1'=2,'shard_0'=8,'shard_1'=4] {'rep_0','rep_1','shar..., dimensions={0} | all-to-all | bytes 278528 | tf_op jit(solution)/shard_map/all_to_all | solution.py:13
  91.1 0.9 broadcast_in_dim.30
  92.0 3.7 %all-to-all-start.4 = ((f32[4,64,544]{2,1,0:T(8,128)}), f32[4,64,544]{2,1,0:T(8,128)S(1)}, u32[]{:S(2)}, u32[]{:S(2)}) async-start(f32[4,64,544]{2,1,0:T(8,128)} %broadcast_in_dim.30), calls=%async_computation.4 | async-start | bytes 1310720 | tf_op jit(solution)/shard_map/all_to_all | solution.py:13
  95.7 8.7 %all-to-all-done.4 = f32[4,64,544]{2,1,0:T(8,128)S(1)} async-done(((f32[4,64,544]{2,1,0:T(8,128)}), f32[4,64,544]{2,1,0:T(8,128)S(1)}, u32[]{:S(2)}, u32[]{:S(2)}) %all-to-all-start.4) | async-done | bytes 557088 | tf_op jit(solution)/shard_map/all_to_all | solution.py:13
  104.4 0.0 copy-start.3
  104.4 0.8 copy-done.3
  105.2 1.5 %copy.34 = f32[64,4,544]{2,1,0:T(4,128)S(1)} copy(f32[64,4,544]{2,0,1:T(8,128)} %bitcast.30) | data formatting | bytes 1114112 | tf_op jit(solution)/shard_map/transpose | solution.py:35
  106.8 1.4 reshape_reshape.7
  108.2 1.9 %slice.23 = f32[34,64,64]{2,1,0:T(8,128)} reshape(f32[64,4,544]{2,1,0:T(4,128)S(1)} %copy.34) | data formatting | bytes 1114112 | tf_op jit(solution)/shard_map/slice | solution.py:66
  110.1 0.0 slice-start
  110.1 0.9 slice.26
  111.0 0.1 copy.46
  111.1 0.9 fusion.11
  111.9 11.7 %custom-call.9 = f32[2,64,64]{2,1,0:T(8,128)S(1)} custom-call(f32[2,64,64]{2,1,0:T(8,128)S(1)} %fusion.11), custom_call_target="Cholesky" | custom-call | tf_op jit(solution)/shard_map/jit(cholesky)/cholesky | solution.py:72
  123.7 0.1 compare_reduce_fusion
  123.8 0.1 select_bitcast_fusion
  123.9 9.8 %custom-call.10 = f32[2,1,64,64]{2,3,1,0:T(8,128)S(1)} custom-call(f32[2,1,64,64]{3,2,1,0:T(8,128)S(1)} %select_bitcast_fusion), custom_call_target="InvertDiagBlocksLowerTriangular" | custom-call | tf_op jit(solution)/shard_map/triangular_solve | solution.py:73
  133.7 0.3 fusion.5
  134.1 0.0 slice-done
  134.1 1.2 reshape.45
  135.2 0.0 copy-start.2
  135.2 2.6 %convolution_multiply_fusion = f32[2,1024,64]{1,2,0:T(8,128)S(1)} fusion(f32[2,1024,64]{2,1,0:T(8,128)} %reshape.45, f32[2,1,64,64]{2,3,1,0:T(8,128)S(1)} %custom-call.10), kind=kOutput, calls=%fused_computation.7 | convolution fusion | flops 100794368 | bytes 1081344 | tf_op jit(solution)/shard_map/triangular_solve | solution.py:90
  137.9 0.0 copy-done.2
  137.9 0.0 copy-start.4
  137.9 3.7 %fusion.4 = (f32[1,2,256,1024]{3,2,1,0:T(8,128)}, bf16[2,256,1024]{2,1,0:T(8,128)(2,1)}) fusion(f32[1,2,256,1024]{3,2,1,0:T(8,128)S(1)} %copy-done.1, bf16[1,2,256,1024]{3,2,1,0:T(8,128)(2,1)S(1)} %copy-done.2, f32[2,256,64]{1,2,0:T(8,128)S(1)} %fusion.5, f32[2,1024,64]{1,2,0:T(8,128)S(1)} %convolution_multiply_fusion), kind=kOutput, calls=%fused_computation.5 | convolution fusion | flops 404750336 | bytes 6946816 | tf_op jit(solution)/shard_map/mrk,mck->mrc/dot_general | solution.py:93
  141.6 0.0 copy-done.4
  (5 shorter events, 0.1 us)
Async XLA Ops:
  0.6 1.0 copy-start
  5.8 23.0 %copy-start.1 = (f32[1,2,256,1024]{3,2,1,0:T(8,128)S(1)}, f32[1,2,256,1024]{3,2,1,0:T(8,128)}, u32[]{:S(2)}) copy-start(f32[1,2,256,1024]{3,2,1,0:T(8,128)} %param.4) | copy-start | bytes 6291460
  92.0 12.4 %all-to-all-start.4 = ((f32[4,64,544]{2,1,0:T(8,128)}), f32[4,64,544]{2,1,0:T(8,128)S(1)}, u32[]{:S(2)}, u32[]{:S(2)}) async-start(f32[4,64,544]{2,1,0:T(8,128)} %broadcast_in_dim.30), calls=%async_computation.4 | async-start | bytes 1310720 | tf_op jit(solution)/shard_map/all_to_all | solution.py:13
  104.4 0.8 copy-start.3
  110.1 24.0 %slice-start = ((f32[139264]{0:T(1024)}), f32[131072]{0:T(1024)S(1)}, s32[]{:S(2)}) async-start(f32[139264]{0:T(1024)} %reshape_reshape.7), calls=%async_computation.5 | async-start | bytes 1048576 | tf_op jit(solution)/shard_map/slice | solution.py:66
  135.2 2.6 %copy-start.2 = (bf16[1,2,256,1024]{3,2,1,0:T(8,128)(2,1)S(1)}, bf16[1,2,256,1024]{3,2,1,0:T(8,128)(2,1)}, u32[]{:S(2)}) copy-start(bf16[1,2,256,1024]{3,2,1,0:T(8,128)(2,1)} %param.3) | copy-start | bytes 3145732
  137.9 3.7 %copy-start.4 = (f32[2,1024,64]{1,2,0:T(8,128)}, f32[2,1024,64]{1,2,0:T(8,128)S(1)}, u32[]{:S(2)}) copy-start(f32[2,1024,64]{1,2,0:T(8,128)S(1)} %convolution_multiply_fusion) | copy-start | bytes 1572868
where the time goes:
time: 143 us; the launch traced here: 142 us
  blocking collectives  72.1 us (50%)
  other arithmetic  25.6 us (18%)
  matrix products  16.7 us (12%)
  local copies, waits for them, and re-layouts  14 us (10%)
  waiting for transfers between devices  8.7 us (6%)
  starting transfers between devices  3.66 us (3%)
    all_to_all x2, blocking collectives, sent_to_all(): lax.all_to_all(jnp.broadcast_to(x[None], (count, *x.shape)), axis, 0, 0,...  37.1 us
    all_to_all x1, blocking collectives, sum_by_axis(): return jnp.sum(lax.all_to_all(own, far, 0, 0, tiled=True), axis=0)  22.2 us
    all_to_all x1, blocking collectives, sum_at_owner(): lax.all_to_all(tiles, axis, split_axis=0, concat_axis=0, tiled=True)  12.7 us
    another operation x4, other arithmetic, orthogonal(): chol = jnp.linalg.cholesky(gram)  11.9 us
    another operation x3, other arithmetic, orthogonal(): lax.linalg.triangular_solve(chol, left, left_side=False, lower=True, tran...  9.92 us
    all_to_all x1, waiting for transfers between devices, sent_to_all(): lax.all_to_all(jnp.broadcast_to(x[None], (count, *x.shape)), axis, 0, 0,...  8.7 us
    dot_general x1, matrix products, on_device(): local_right = jnp.einsum('mrc,mrk->mck', merged, left, precision=highest)  5.63 us
    dot_general x1, matrix products, on_device(): local_left = jnp.einsum('mrc,mck->mrk', merged, basis_kv, precision=highest)  4.12 us
  transfers between devices with their start and end apart: 1, of which 1 were waited for; matrix products, arithmetic and copies ran while one was open for 0% of the time, Pallas kernels for 0%

commit v1 on v0

v1 whole, which is shorter than its diff:
```python
import functools

import jax
import jax.numpy as jnp
from jax import lax
from jax.experimental import pallas as pl
from jax.experimental.pallas import tpu as pltpu
from jax.sharding import PartitionSpec as P

MESH = pl.DeviceIdType.MESH
F32 = jnp.float32
BF16 = jnp.bfloat16
HIGHEST = lax.Precision.HIGHEST

ROWS = 256
KVC = 1024
RANK = 64
NX, NY, NZ = 4, 4, 8
NQ = 4
QR = ROWS // NQ
NCH = 2
CW = KVC // NCH
PW = CW // 2
PLANE = [(dx, dy) for dx in range(NX) for dy in range(NY) if dx or dy]


def split(x):
    hi = x.astype(BF16)
    return hi, (x - hi.astype(F32)).astype(BF16)


def nt(a, b, **kw):
    return lax.dot_general(a, b, (((1,), (1,)), ((), ())), preferred_element_type=F32, **kw)


def nn(a, b, **kw):
    return lax.dot_general(a, b, (((1,), (0,)), ((), ())), preferred_element_type=F32, **kw)


def factor_panels(blocks, panels):
    sub_i = lax.broadcasted_iota(jnp.int32, (8, 128), 0)
    for kb in panels:
        live = range(kb, 8)
        cols = {
            b: [jnp.broadcast_to(blocks[b][:, 8 * kb + j : 8 * kb + j + 1], (8, 128)) for j in range(8)]
            for b in live
        }
        for s in range(8):
            row = jnp.broadcast_to(blocks[kb][s : s + 1, :], (8, 128))
            inv = 1.0 / jnp.broadcast_to(cols[kb][s][s : s + 1, :], (8, 128))
            heads = [jnp.broadcast_to(cols[kb][j][s : s + 1, :], (8, 128)) for j in range(8)]
            for b in live:
                f = cols[b][s] * inv
                if b == kb:
                    f = jnp.where(sub_i > s, f, 0.0)
                blocks[b] = blocks[b] - f * row
                for j in range(s + 1, 8):
                    cols[b][j] = cols[b][j] - f * heads[j]
    return blocks


def comm_kernel(
    grad_ref, err_ref, basis_ref,
    rt_out, cinv_out, ot_out,
    g_o, e_o, g_s, e_s, b_v, mo, pin, p_hi, p_lo,
    l1, lr1, l2, lr2,
    gz_b, gz_r, gx_b, gx_r,
    rs_b, rs_r, z_b, z_r, ag_b, w_b,
    ld, px_s, px_r, l_s, l_r, g_ss, g_rs, rs_s, rs_rs, z_s, z_rs, ag_s, ag_rs, fw_s, fw_r, co_s, co_r,
):
    rep, shard = lax.axis_index("rep"), lax.axis_index("shard")
    y, c = rep // 2, rep % 2
    z, x = shard // NX, shard % NX

    def dev(yy, zz, xx, cc=None):
        return (yy * 2 + (c if cc is None else cc), zz * NX + xx)

    partner = dev(y, z, x, 1 - c)
    plane = [(dx, dy, dev((y + dy) % NY, z, (x + dx) % NX)) for dx, dy in PLANE]
    zline = [dev(y, (z + d) % NZ, x) for d in range(1, NZ)]
    xline = [dev(y, z, (x + d) % NX) for d in range(1, NX)]

    def remote(src, dst, ss, rs, to):
        copy = pltpu.make_async_remote_copy(
            src_ref=src, dst_ref=dst, send_sem=ss, recv_sem=rs, device_id=to, device_id_type=MESH
        )
        copy.start()
        return copy

    def wait_bytes(ref, sem):
        pltpu.make_async_copy(ref, ref, sem).wait()

    oc = 1 - c
    loads = []
    for q in range(NQ):
        rows = pl.ds(q * QR, QR)
        pair = []
        for k, (hbm, buf) in enumerate(((grad_ref, g_o), (err_ref, e_o))):
            cp = pltpu.make_async_copy(hbm.at[oc, rows, :], buf.at[rows, :], ld.at[2 * q + k])
            cp.start()
            pair.append(cp)
        loads.append(pair)
    own_b = pltpu.make_async_copy(basis_ref.at[c], b_v, ld.at[2 * NQ])
    own_b.start()
    own_g = pltpu.make_async_copy(grad_ref.at[c], g_s, ld.at[2 * NQ + 1])
    own_g.start()
    own_e = pltpu.make_async_copy(err_ref.at[c], e_s, ld.at[2 * NQ + 2])
    own_e.start()

    barrier = pltpu.get_barrier_semaphore()
    peers = [partner] + [d for _, _, d in plane] + zline
    for d in peers:
        pl.semaphore_signal(barrier, inc=1, device_id=d, device_id_type=MESH)
    pl.semaphore_wait(barrier, len(peers))

    px = []
    for q in range(NQ):
        rows = pl.ds(q * QR, QR)
        loads[q][0].wait()
        loads[q][1].wait()
        mo[q] = g_o[rows, :].astype(F32) + e_o[rows, :]
        px.append(remote(mo.at[q], pin.at[q], px_s.at[q], px_r.at[q], partner))
    own_b.wait()
    bt = b_v[...].T
    bt_h, bt_l = split(bt)
    bt2 = jnp.concatenate([bt_h, bt_l], axis=0)
    own_g.wait()
    own_e.wait()
    for q in range(NQ):
        rows = pl.ds(q * QR, QR)
        px[q].wait_recv()
        p = g_s[rows, :].astype(F32) + e_s[rows, :] + pin[q]
        h, l = split(p)
        p_hi[rows, :] = h
        p_lo[rows, :] = l

    ph = p_hi[...]
    pw = p_lo[...]
    t = nt(bt2, ph)
    lt = (t[:RANK] + t[RANK:] + nt(bt_h, pw)) * 0.125
    l1[...] = lt
    flip = y + 1 - 2 * (y % 2)
    side = (y + 3 + 2 * (y % 2)) % NY
    d_flip, d_side = dev(flip, z, x), dev(side, z, x)
    half = RANK // 2
    lo_half, hi_half = pl.ds(0, half), pl.ds(half, half)
    a1 = remote(l1.at[lo_half], lr1.at[lo_half], l_s.at[0], l_r.at[0], d_flip)
    b1 = remote(l1.at[hi_half], lr1.at[hi_half], l_s.at[1], l_r.at[1], d_side)
    a1.wait_recv()
    l2[lo_half, :] = lt[:half] + lr1[lo_half, :]
    a2 = remote(l2.at[lo_half], lr2.at[lo_half], l_s.at[2], l_r.at[2], d_side)
    b1.wait_recv()
    l2[hi_half, :] = lt[half:] + lr1[hi_half, :]
    b2 = remote(l2.at[hi_half], lr2.at[hi_half], l_s.at[3], l_r.at[3], d_flip)
    a2.wait_recv()
    b2.wait_recv()
    lt = l2[...] + lr2[...]

    gram = nt(lt, lt, precision=HIGHEST)
    gz_b[...] = jnp.concatenate([gram[: RANK // 2], gram[RANK // 2 :]], axis=1)
    gz = [remote(gz_b, gz_r.at[d], g_ss.at[0], g_rs.at[0], to) for d, to in enumerate(zline)]

    lt_h, lt_l = split(lt)
    lt2 = jnp.concatenate([lt_h, lt_l], axis=0)

    def piece(ref, p, j):
        rows = pl.ds(pl.multiple_of((p // 2) * 8, 8), 8)
        cols = pl.ds(pl.multiple_of(j * CW + (p % 2) * PW, PW), PW)
        return rows, cols

    me = y * NX + x
    for j in range(NCH):
        t = nn(lt2, p_hi[:, j * CW : (j + 1) * CW])
        rs_b[:, j * CW : (j + 1) * CW] = t[:RANK] + t[RANK:] + nn(lt_h, p_lo[:, j * CW : (j + 1) * CW])
        for i, (dx, dy, to) in enumerate(plane):
            at = ((y + dy) % NY) * NX + (x + dx) % NX
            rows, cols = piece(rs_b, at, j)
            remote(rs_b.at[rows, cols], rs_r.at[j, i], rs_s.at[j], rs_rs.at[j], to)

    def gram_z():
        wait_bytes(gz_r, g_rs.at[0])
        r = [gz_b[...]] + [gz_r[d] for d in range(NZ - 1)]
        gx_b[...] = ((r[0] + r[4]) + (r[2] + r[6])) + ((r[1] + r[5]) + (r[3] + r[7]))
        for d, to in enumerate(xline):
            remote(gx_b, gx_r.at[d], g_ss.at[1], g_rs.at[1], to)

    def sum_rs(j):
        wait_bytes(rs_r.at[j], rs_rs.at[j])
        rows, cols = piece(rs_b, me, j)
        r = [rs_b[rows, cols]] + [rs_r[j, i] for i in range(len(PLANE))]
        while len(r) > 1:
            r = [r[i] + r[i + 1] for i in range(0, len(r), 2)]
        z_b[j] = r[0]
        for d, to in enumerate(zline):
            remote(z_b.at[j], z_r.at[j, d], z_s.at[j], z_rs.at[j], to)

    def sum_z(j):
        wait_bytes(z_r.at[j], z_rs.at[j])
        r = [z_b[j]] + [z_r[j, d] for d in range(NZ - 1)]
        total = ((r[0] + r[4]) + (r[2] + r[6])) + ((r[1] + r[5]) + (r[3] + r[7]))
        rows, cols = piece(rs_b, me, j)
        ag_b[j] = total
        rt_out[c, rows, cols] = total
        for _, _, to in plane:
            remote(ag_b.at[j], rt_out.at[c, rows, cols], ag_s.at[j], ag_rs.at[j], to)

    sum_rs(0)
    gram_z()
    for j in range(1, NCH):
        sum_rs(j)
    wait_bytes(gx_r, g_rs.at[1])
    g = (gx_b[...] + gx_r[1]) + (gx_r[0] + gx_r[2])
    gram = jnp.concatenate([g[:, :RANK], g[:, RANK:]], axis=0)
    ri = lax.broadcasted_iota(jnp.int32, (RANK, RANK), 0)
    ci = lax.broadcasted_iota(jnp.int32, (RANK, RANK), 1)
    w = jnp.concatenate([gram, jnp.where(ri == ci, 1.0, 0.0)], axis=1)
    blocks = [w[8 * b : 8 * b + 8] for b in range(8)]
    blocks = factor_panels(blocks, range(0, 2))
    for j in range(NCH):
        sum_z(j)
    blocks = factor_panels(blocks, range(2, 8))
    w = jnp.concatenate(blocks, axis=0)
    u, low = w[:, :RANK], w[:, RANK:]
    diag = jnp.sum(jnp.where(ri == ci, u, 0.0), axis=1, keepdims=True)
    cinv = low * lax.rsqrt(diag)
    w_b[...] = jnp.concatenate([cinv, jnp.zeros_like(cinv)], axis=1)
    cinv_out[c] = w_b[...]
    ot_out[c] = nn(cinv, lt, precision=HIGHEST)
    remote(cinv_out.at[c], cinv_out.at[c], co_s.at[0], co_r.at[0], partner)
    remote(ot_out.at[c], ot_out.at[c], co_s.at[1], co_r.at[1], partner)
    for j in range(NCH):
        wait_bytes(rs_r.at[j], ag_rs.at[j])
        cols = pl.ds(j * CW, CW)
        remote(rt_out.at[c, :, cols], rt_out.at[c, :, cols], fw_s.at[j], fw_r.at[j], partner)

    wait_bytes(cinv_out.at[oc], co_r.at[0])
    wait_bytes(ot_out.at[oc], co_r.at[1])
    for j in range(NCH):
        wait_bytes(rt_out.at[oc, :, pl.ds(j * CW, CW)], fw_r.at[j])
    for q in range(NQ):
        px[q].wait_send()
    for cp in (a1, b1, a2, b2):
        cp.wait_send()
    wait_bytes(gz_r, g_ss.at[0])
    wait_bytes(gx_r, g_ss.at[1])
    for j in range(NCH):
        wait_bytes(rs_r.at[j], rs_s.at[j])
        wait_bytes(z_r.at[j], z_s.at[j])
        wait_bytes(rs_r.at[j], ag_s.at[j])
        wait_bytes(rt_out.at[c, :, pl.ds(j * CW, CW)], fw_s.at[j])
    wait_bytes(cinv_out.at[c], co_s.at[0])
    wait_bytes(ot_out.at[c], co_s.at[1])


RB = 128


def out_kernel(grad_ref, err_ref, rt_ref, cinv_ref, ot_ref, upd_ref, new_ref, next_ref, r3, o3):
    i = pl.program_id(1)

    @pl.when(i == 0)
    def _():
        ch, cl = split(cinv_ref[0][:, :RANK] * 0.125)
        rh, rl = split(rt_ref[0])
        right = nn(jnp.concatenate([ch, cl], axis=1), jnp.concatenate([rh, rh], axis=0)) + nn(ch, rl)
        h, l = split(right)
        r3[0:RANK] = h
        r3[RANK : 2 * RANK] = h
        r3[2 * RANK :] = l
        next_ref[0] = right.T
        oh, ol = split(ot_ref[0].T)
        o3[...] = jnp.concatenate([oh, ol, oh], axis=1)

    approx = nn(o3[pl.ds(i * RB, RB), :], r3[...])
    upd_ref[0] = approx.astype(BF16)
    new_ref[0] = grad_ref[0].astype(F32) + err_ref[0] - approx


def on_device(grad_kv, error_kv, basis_kv):
    grad, err = grad_kv[0], error_kv[0]
    dma = pltpu.SemaphoreType.DMA
    anyspec = pl.BlockSpec(memory_space=pl.ANY)
    vspec = pl.BlockSpec(memory_space=pltpu.VMEM)
    rt, cinv, ot = pl.pallas_call(
        comm_kernel,
        name="exchange",
        out_shape=(
            jax.ShapeDtypeStruct((2, RANK, KVC), F32),
            jax.ShapeDtypeStruct((2, RANK, 128), F32),
            jax.ShapeDtypeStruct((2, RANK, ROWS), F32),
        ),
        in_specs=[anyspec] * 3,
        out_specs=(vspec,) * 3,
        scratch_shapes=[
            pltpu.VMEM((ROWS, KVC), BF16),
            pltpu.VMEM((ROWS, KVC), F32),
            pltpu.VMEM((ROWS, KVC), BF16),
            pltpu.VMEM((ROWS, KVC), F32),
            pltpu.VMEM((KVC, RANK), F32),
            pltpu.VMEM((NQ, QR, KVC), F32),
            pltpu.VMEM((NQ, QR, KVC), F32),
            pltpu.VMEM((ROWS, KVC), BF16),
            pltpu.VMEM((ROWS, KVC), BF16),
            pltpu.VMEM((RANK, ROWS), F32),
            pltpu.VMEM((RANK, ROWS), F32),
            pltpu.VMEM((RANK, ROWS), F32),
            pltpu.VMEM((RANK, ROWS), F32),
            pltpu.VMEM((RANK // 2, 128), F32),
            pltpu.VMEM((NZ - 1, RANK // 2, 128), F32),
            pltpu.VMEM((RANK // 2, 128), F32),
            pltpu.VMEM((NX - 1, RANK // 2, 128), F32),
            pltpu.VMEM((RANK, KVC), F32),
            pltpu.VMEM((NCH, len(PLANE), 8, PW), F32),
            pltpu.VMEM((NCH, 8, PW), F32),
            pltpu.VMEM((NCH, NZ - 1, 8, PW), F32),
            pltpu.VMEM((NCH, 8, PW), F32),
            pltpu.VMEM((RANK, 128), F32),
            dma((2 * NQ + 3,)),
            dma((NQ,)),
            dma((NQ,)),
            dma((4,)),
            dma((4,)),
            dma((2,)),
            dma((2,)),
        ]
        + [dma((NCH,))] * 8
        + [dma((2,)), dma((2,))],
        compiler_params=pltpu.CompilerParams(
            collective_id=0, has_side_effects=True, vmem_limit_bytes=40 << 20
        ),
    )(grad, err, basis_kv)
    whole = lambda shape: pl.BlockSpec((1, *shape), lambda m, i: (m, 0, 0))
    tile = pl.BlockSpec((1, RB, KVC), lambda m, i: (m, i, 0))
    upd, new, nxt = pl.pallas_call(
        out_kernel,
        name="decompress",
        grid=(2, ROWS // RB),
        out_shape=(
            jax.ShapeDtypeStruct((2, ROWS, KVC), BF16),
            jax.ShapeDtypeStruct((2, ROWS, KVC), F32),
            jax.ShapeDtypeStruct((2, KVC, RANK), F32),
        ),
        in_specs=[tile, tile, whole((RANK, KVC)), whole((RANK, 128)), whole((RANK, ROWS))],
        out_specs=(tile, tile, whole((KVC, RANK))),
        scratch_shapes=[pltpu.VMEM((3 * RANK, KVC), BF16), pltpu.VMEM((ROWS, 3 * RANK), BF16)],
    )(grad, err, rt, cinv, ot)
    return upd, new[None], nxt


def solution(mesh):
    placed = (P("rep", None, "shard", None), P("rep", None, "shard", None), P())
    return jax.shard_map(
        on_device,
        mesh=mesh,
        in_specs=placed,
        out_specs=(P(None, "shard", None), P("rep", None, "shard", None), P()),
        check_vma=False,
    )
```

time: 143 us -> 54.2 us (0.38)
  blocking collectives: 72.1 us -> 0 us
  Pallas kernels: 0 us -> 45.8 us
  other arithmetic: 25.6 us -> 0 us
  matrix products: 16.7 us -> 0 us
  waiting for transfers between devices: 8.7 us -> 0 us
  local copies, waits for them, and re-layouts: 14 us -> 7.44 us
  starting transfers between devices: 3.66 us -> 0 us
    all_to_all x4 -> x0, blocking collectives: 72.1 us -> none  [the longest x2 37.1 us: sent_to_all(): lax.all_to_all(jnp.broadcast_to(x[None], (count, *x.shape)), axis, 0, 0,...]
    pallas_call x0 -> x2, Pallas kernels: none -> 45.8 us  [the longest x1 39.9 us: on_device(): pl.pallas_call(comm_kernel, name='exchange', out_shape=(jax.ShapeDtypeStr...]
    another operation x7 -> x0, other arithmetic: 21.8 us -> none  [the longest x4 11.9 us: orthogonal(): chol = jnp.linalg.cholesky(gram)]
    dot_general x4 -> x0, matrix products: 13.7 us -> none  [the longest x1 5.63 us: on_device(): local_right = jnp.einsum('mrc,mrk->mck', merged, left, precision=highest)]
    all_to_all x1 -> x0, waiting for transfers between devices: 8.7 us -> none  [sent_to_all(): lax.all_to_all(jnp.broadcast_to(x[None], (count, *x.shape)), axis, 0, 0,...]
    unnamed x12, local copies, waits for them, and re-layouts: 1.98 us -> 7.44 us
    all_to_all x1 -> x0, starting transfers between devices: 3.66 us -> none  [sent_to_all(): lax.all_to_all(jnp.broadcast_to(x[None], (count, *x.shape)), axis, 0, 0,...]
    another operation x2 -> x0, matrix products: 2.95 us -> none  [the longest x1 2.61 us: on_device(): lax.linalg.triangular_solve(chol, summed, left_side=False, lower=True, tr...]
  transfers between devices with their start and end apart: 1 -> 0, of which waited for: 1 -> 0; matrix products, arithmetic and copies ran while one was open for 0% -> 0% of each run, Pallas kernels for 0% -> 0%
where the time goes in v1:
time: 54.2 us; the launch traced here: 54 us
  Pallas kernels  45.8 us (85%)
  local copies, waits for them, and re-layouts  7.44 us (14%)
  between operations  0.68 us (1%)
    pallas_call x1, Pallas kernels, on_device(): pl.pallas_call(comm_kernel, name='exchange', out_shape=(jax.ShapeDtypeStr...  39.9 us
    unnamed x12, local copies, waits for them, and re-layouts  7.44 us
    pallas_call x1, Pallas kernels, on_device(): pl.pallas_call(out_kernel, name='decompress', grid=(2, ROWS // RB), out_s...  5.96 us

profile of v1, /device:TPU:1, one launch (start us, length us, event | category | flops | bytes accessed | tf_op | source)
XLA Modules:
  0.0 54.0 jit_solution(16662229504548059352)
XLA Ops:
  0.6 0.0 copy-start.1
  0.6 1.5 %copy.6.basis_ref = f32[2,1024,64]{2,1,0:T(8,128)S(1)} copy(f32[2,1024,64]{1,2,0:T(8,128)} %param.5) | data formatting | bytes 1048576 | tf_op args[2]
  2.1 0.0 copy-done.1
  2.1 0.0 copy-start
  2.1 1.6 %copy-done = f32[1,2,256,1024]{3,2,1,0:T(8,128)S(1)} copy-done((f32[1,2,256,1024]{3,2,1,0:T(8,128)S(1)}, f32[1,2,256,1024]{3,2,1,0:T(8,128)}, u32[]{:S(2)}) %copy-start) | copy-done | bytes 2097176
  3.7 39.9 %exchange.1 = (f32[2,64,1024]{2,1,0:T(8,128)S(1)}, f32[2,64,128]{2,1,0:T(8,128)S(1)}, f32[2,64,256]{2,1,0:T(8,128)S(1)}) custom-call(bf16[2,256,1024]{2,1,0:T(8,128)(2,1)S(1)} %bitcast.6, f32[2,256,1024]{2,1,0:T(8,128)S(1)} %bitcast.4, f32[2,1024,64]{2,1,0:T(8,128)S(1)} %copy.6.basis_ref), custom_call_target="tpu_custom_call" | custom-call | tf_op jit(solution)/shard_map/exchange/pallas_call | solution.py:284
  43.6 0.0 copy-start.2
  43.6 0.8 %copy-done.2 = f32[2,64,1024]{2,1,0:T(8,128)} copy-done((f32[2,64,1024]{2,1,0:T(8,128)}, f32[2,64,1024]{2,1,0:T(8,128)S(1)}, u32[]{:S(2)}) %copy-start.2) | copy-done | bytes 524312
  44.4 0.0 copy-start.3
  44.4 0.7 %copy-done.3 = f32[2,64,256]{2,1,0:T(8,128)} copy-done((f32[2,64,256]{2,1,0:T(8,128)}, f32[2,64,256]{2,1,0:T(8,128)S(1)}, u32[]{:S(2)}) %copy-start.3) | copy-done | bytes 131096
  45.0 0.0 copy-start.4
  45.1 0.6 %copy-done.4 = f32[2,64,128]{2,1,0:T(8,128)} copy-done((f32[2,64,128]{2,1,0:T(8,128)}, f32[2,64,128]{2,1,0:T(8,128)S(1)}, u32[]{:S(2)}) %copy-start.4) | copy-done | bytes 65560
  45.7 6.0 %decompress.1 = (bf16[2,256,1024]{2,1,0:T(8,128)(2,1)}, f32[2,256,1024]{2,1,0:T(8,128)}, f32[2,1024,64]{2,1,0:T(8,128)}) custom-call(bf16[2,256,1024]{2,1,0:T(8,128)(2,1)} %bitcast.5, f32[2,256,1024]{2,1,0:T(8,128)} %bitcast.3, f32[2,64,1024]{2,1,0:T(8,128)} %copy-done.2, f32[2,64,128]{2,1,0:T(8,128)} %copy-done.4, f32[2,64,256]{2,1,0:T(8,128)} %copy-done.3), custom_call_target="tpu_custom_call" | custom-call | tf_op jit(solution)/shard_map/decompress/pallas_call | solution.py:334
  51.6 2.3 %copy.7 = f32[2,1024,64]{1,2,0:T(8,128)} copy(f32[2,1024,64]{2,1,0:T(8,128)} %get-tuple-element.17) | data formatting | bytes 1048576
Async XLA Ops:
  0.6 1.5 %copy-start.1 = (bf16[1,2,256,1024]{3,2,1,0:T(8,128)(2,1)S(1)}, bf16[1,2,256,1024]{3,2,1,0:T(8,128)(2,1)}, u32[]{:S(2)}) copy-start(bf16[1,2,256,1024]{3,2,1,0:T(8,128)(2,1)} %param.3) | copy-start | bytes 3145732
  2.1 1.6 %copy-start = (f32[1,2,256,1024]{3,2,1,0:T(8,128)S(1)}, f32[1,2,256,1024]{3,2,1,0:T(8,128)}, u32[]{:S(2)}) copy-start(f32[1,2,256,1024]{3,2,1,0:T(8,128)} %param.4) | copy-start | bytes 6291460
  43.6 0.8 %copy-start.2 = (f32[2,64,1024]{2,1,0:T(8,128)}, f32[2,64,1024]{2,1,0:T(8,128)S(1)}, u32[]{:S(2)}) copy-start(f32[2,64,1024]{2,1,0:T(8,128)S(1)} %get-tuple-element.9.rt_ref) | copy-start | bytes 1572868
  44.4 0.7 %copy-start.3 = (f32[2,64,256]{2,1,0:T(8,128)}, f32[2,64,256]{2,1,0:T(8,128)S(1)}, u32[]{:S(2)}) copy-start(f32[2,64,256]{2,1,0:T(8,128)S(1)} %get-tuple-element.11.ot_ref) | copy-start | bytes 393220
  45.0 0.6 %copy-start.4 = (f32[2,64,128]{2,1,0:T(8,128)}, f32[2,64,128]{2,1,0:T(8,128)S(1)}, u32[]{:S(2)}) copy-start(f32[2,64,128]{2,1,0:T(8,128)S(1)} %get-tuple-element.10.cinv_ref) | copy-start | bytes 196612

commit v2 on v1

--- a/solution.py
+++ b/solution.py
@@ -61,12 +61,13 @@
 
 def comm_kernel(
     grad_ref, err_ref, basis_ref,
-    rt_out, cinv_out, ot_out,
-    g_o, e_o, g_s, e_s, b_v, mo, pin, p_hi, p_lo,
+    rt_out, cinv_out, ot_out, mer,
+    g_o, e_o, g_s, e_s, b_v, pin, p_hi, p_lo,
     l1, lr1, l2, lr2,
     gz_b, gz_r, gx_b, gx_r,
     rs_b, rs_r, z_b, z_r, ag_b, w_b,
     ld, px_s, px_r, l_s, l_r, g_ss, g_rs, rs_s, rs_rs, z_s, z_rs, ag_s, ag_rs, fw_s, fw_r, co_s, co_r,
+    near2, near3, near4,
 ):
     rep, shard = lax.axis_index("rep"), lax.axis_index("shard")
     y, c = rep // 2, rep % 2
@@ -107,37 +108,44 @@
     own_e = pltpu.make_async_copy(err_ref.at[c], e_s, ld.at[2 * NQ + 2])
     own_e.start()
 
+    near = [
+        dev(y, z, (x + 1) % NX), dev(y, z, (x + NX - 1) % NX),
+        dev((y + 1) % NY, z, x), dev((y + NY - 1) % NY, z, x),
+        dev(y, (z + 1) % NZ, x), dev(y, (z + NZ - 1) % NZ, x),
+    ]
+
+    def tell(sem, peers):
+        for d in peers:
+            pl.semaphore_signal(sem, inc=1, device_id=d, device_id_type=MESH)
+
     barrier = pltpu.get_barrier_semaphore()
-    peers = [partner] + [d for _, _, d in plane] + zline
-    for d in peers:
-        pl.semaphore_signal(barrier, inc=1, device_id=d, device_id_type=MESH)
-    pl.semaphore_wait(barrier, len(peers))
+    tell(barrier, [partner] + near)
+    pl.semaphore_wait(barrier, 1 + len(near))
+    tell(near2, near)
 
     px = []
     for q in range(NQ):
         rows = pl.ds(q * QR, QR)
         loads[q][0].wait()
         loads[q][1].wait()
-        mo[q] = g_o[rows, :].astype(F32) + e_o[rows, :]
-        px.append(remote(mo.at[q], pin.at[q], px_s.at[q], px_r.at[q], partner))
+        mer[oc, rows, :] = g_o[rows, :].astype(F32) + e_o[rows, :]
+        px.append(remote(mer.at[oc, rows, :], pin.at[rows, :], px_s.at[q], px_r.at[q], partner))
     own_b.wait()
-    bt = b_v[...].T
-    bt_h, bt_l = split(bt)
+    bt_h, bt_l = split(b_v[...])
     bt2 = jnp.concatenate([bt_h, bt_l], axis=0)
     own_g.wait()
     own_e.wait()
+    mer[c] = g_s[...].astype(F32) + e_s[...]
+    pl.semaphore_wait(near2, len(near))
+    tell(near3, near)
     for q in range(NQ):
         rows = pl.ds(q * QR, QR)
         px[q].wait_recv()
-        p = g_s[rows, :].astype(F32) + e_s[rows, :] + pin[q]
-        h, l = split(p)
+        h, l = split(mer[c, rows, :] + pin[rows, :])
         p_hi[rows, :] = h
         p_lo[rows, :] = l
-
-    ph = p_hi[...]
-    pw = p_lo[...]
-    t = nt(bt2, ph)
-    lt = (t[:RANK] + t[RANK:] + nt(bt_h, pw)) * 0.125
+    t = nt(bt2, p_hi[...])
+    lt = (t[:RANK] + t[RANK:] + nt(bt_h, p_lo[...])) * 0.125
     l1[...] = lt
     flip = y + 1 - 2 * (y % 2)
     side = (y + 3 + 2 * (y % 2)) % NY
@@ -146,6 +154,8 @@
     lo_half, hi_half = pl.ds(0, half), pl.ds(half, half)
     a1 = remote(l1.at[lo_half], lr1.at[lo_half], l_s.at[0], l_r.at[0], d_flip)
     b1 = remote(l1.at[hi_half], lr1.at[hi_half], l_s.at[1], l_r.at[1], d_side)
+    pl.semaphore_wait(near3, len(near))
+    tell(near4, near)
     a1.wait_recv()
     l2[lo_half, :] = lt[:half] + lr1[lo_half, :]
     a2 = remote(l2.at[lo_half], lr2.at[lo_half], l_s.at[2], l_r.at[2], d_side)
@@ -155,6 +165,7 @@
     a2.wait_recv()
     b2.wait_recv()
     lt = l2[...] + lr2[...]
+    pl.semaphore_wait(near4, len(near))
 
     gram = nt(lt, lt, precision=HIGHEST)
     gz_b[...] = jnp.concatenate([gram[: RANK // 2], gram[RANK // 2 :]], axis=1)
@@ -252,53 +263,64 @@
     wait_bytes(ot_out.at[c], co_s.at[1])
 
 
-RB = 128
-
-
-def out_kernel(grad_ref, err_ref, rt_ref, cinv_ref, ot_ref, upd_ref, new_ref, next_ref, r3, o3):
-    i = pl.program_id(1)
-
-    @pl.when(i == 0)
-    def _():
-        ch, cl = split(cinv_ref[0][:, :RANK] * 0.125)
-        rh, rl = split(rt_ref[0])
+OB = 64
+
+
+def out_kernel(mer_ref, rt_ref, cinv_ref, ot_ref, upd_ref, new_ref, next_ref, upd, new, nxt, r3, o3, sems):
+    started = []
+
+    def out(src, dst, sem):
+        copy = pltpu.make_async_copy(src, dst, sem)
+        copy.start()
+        started.append(copy)
+
+    for m in range(2):
+        ch, cl = split(cinv_ref[m][:, :RANK] * 0.125)
+        rh, rl = split(rt_ref[m])
         right = nn(jnp.concatenate([ch, cl], axis=1), jnp.concatenate([rh, rh], axis=0)) + nn(ch, rl)
+        nxt[m] = right
+        out(nxt.at[m], next_ref.at[m], sems.at[0, m])
         h, l = split(right)
-        r3[0:RANK] = h
-        r3[RANK : 2 * RANK] = h
-        r3[2 * RANK :] = l
-        next_ref[0] = right.T
-        oh, ol = split(ot_ref[0].T)
-        o3[...] = jnp.concatenate([oh, ol, oh], axis=1)
-
-    approx = nn(o3[pl.ds(i * RB, RB), :], r3[...])
-    upd_ref[0] = approx.astype(BF16)
-    new_ref[0] = grad_ref[0].astype(F32) + err_ref[0] - approx
+        r3[m, 0:RANK] = h
+        r3[m, RANK : 2 * RANK] = h
+        r3[m, 2 * RANK :] = l
+        oh, ol = split(ot_ref[m].T)
+        o3[m] = jnp.concatenate([oh, ol, oh], axis=1)
+        for i in range(ROWS // OB):
+            rows = pl.ds(i * OB, OB)
+            approx = nn(o3[m, rows, :], r3[m])
+            upd[m, rows, :] = approx.astype(BF16)
+            new[m, rows, :] = mer_ref[m, rows, :] - approx
+            n = m * (ROWS // OB) + i
+            out(upd.at[m, rows, :], upd_ref.at[m, rows, :], sems.at[1, n])
+            out(new.at[m, rows, :], new_ref.at[m, rows, :], sems.at[2, n])
+    for copy in started:
+        copy.wait()
 
 
 def on_device(grad_kv, error_kv, basis_kv):
     grad, err = grad_kv[0], error_kv[0]
     dma = pltpu.SemaphoreType.DMA
-    anyspec = pl.BlockSpec(memory_space=pl.ANY)
+    anyspec = pl.BlockSpec(memory_space=pltpu.HBM)
     vspec = pl.BlockSpec(memory_space=pltpu.VMEM)
-    rt, cinv, ot = pl.pallas_call(
+    rt, cinv, ot, mer = pl.pallas_call(
         comm_kernel,
         name="exchange",
         out_shape=(
             jax.ShapeDtypeStruct((2, RANK, KVC), F32),
             jax.ShapeDtypeStruct((2, RANK, 128), F32),
             jax.ShapeDtypeStruct((2, RANK, ROWS), F32),
+            jax.ShapeDtypeStruct((2, ROWS, KVC), F32),
         ),
         in_specs=[anyspec] * 3,
-        out_specs=(vspec,) * 3,
+        out_specs=(vspec,) * 4,
         scratch_shapes=[
             pltpu.VMEM((ROWS, KVC), BF16),
             pltpu.VMEM((ROWS, KVC), F32),
             pltpu.VMEM((ROWS, KVC), BF16),
             pltpu.VMEM((ROWS, KVC), F32),
-            pltpu.VMEM((KVC, RANK), F32),
-            pltpu.VMEM((NQ, QR, KVC), F32),
-            pltpu.VMEM((NQ, QR, KVC), F32),
+            pltpu.VMEM((RANK, KVC), F32),
+            pltpu.VMEM((ROWS, KVC), F32),
             pltpu.VMEM((ROWS, KVC), BF16),
             pltpu.VMEM((ROWS, KVC), BF16),
             pltpu.VMEM((RANK, ROWS), F32),
@@ -324,27 +346,33 @@
             dma((2,)),
         ]
         + [dma((NCH,))] * 8
-        + [dma((2,)), dma((2,))],
+        + [dma((2,)), dma((2,))]
+        + [pltpu.SemaphoreType.REGULAR] * 3,
         compiler_params=pltpu.CompilerParams(
             collective_id=0, has_side_effects=True, vmem_limit_bytes=40 << 20
         ),
-    )(grad, err, basis_kv)
-    whole = lambda shape: pl.BlockSpec((1, *shape), lambda m, i: (m, 0, 0))
-    tile = pl.BlockSpec((1, RB, KVC), lambda m, i: (m, i, 0))
+    )(*(pltpu.with_memory_space_constraint(a, pltpu.HBM) for a in (grad, err, jnp.swapaxes(basis_kv, 1, 2))))
     upd, new, nxt = pl.pallas_call(
         out_kernel,
         name="decompress",
-        grid=(2, ROWS // RB),
         out_shape=(
             jax.ShapeDtypeStruct((2, ROWS, KVC), BF16),
             jax.ShapeDtypeStruct((2, ROWS, KVC), F32),
-            jax.ShapeDtypeStruct((2, KVC, RANK), F32),
+            jax.ShapeDtypeStruct((2, RANK, KVC), F32),
         ),
-        in_specs=[tile, tile, whole((RANK, KVC)), whole((RANK, 128)), whole((RANK, ROWS))],
-        out_specs=(tile, tile, whole((KVC, RANK))),
-        scratch_shapes=[pltpu.VMEM((3 * RANK, KVC), BF16), pltpu.VMEM((ROWS, 3 * RANK), BF16)],
-    )(grad, err, rt, cinv, ot)
-    return upd, new[None], nxt
+        in_specs=[vspec] * 4,
+        out_specs=(anyspec,) * 3,
+        scratch_shapes=[
+            pltpu.VMEM((2, ROWS, KVC), BF16),
+            pltpu.VMEM((2, ROWS, KVC), F32),
+            pltpu.VMEM((2, RANK, KVC), F32),
+            pltpu.VMEM((2, 3 * RANK, KVC), BF16),
+            pltpu.VMEM((2, ROWS, 3 * RANK), BF16),
+            dma((3, 2 * ROWS // OB)),
+        ],
+        compiler_params=pltpu.CompilerParams(vmem_limit_bytes=16 << 20),
+    )(mer, rt, cinv, ot)
+    return upd, new[None], jnp.swapaxes(nxt, 1, 2)
 
 
 def solution(mesh):

time: 54.2 us -> 41.5 us (0.77)
  local copies, waits for them, and re-layouts: 7.44 us -> 0 us
  Pallas kernels: 45.8 us -> 40.8 us
    unnamed x12 -> x0, local copies, waits for them, and re-layouts: 7.44 us -> none
    pallas_call x1, Pallas kernels: 5.96 us -> 2.4 us  [on_device(): pl.pallas_call(out_kernel, name='decompress', out_shape=(jax.ShapeDtypeSt...]
    pallas_call x1, Pallas kernels: 39.9 us -> 38.4 us  [on_device(): pl.pallas_call(comm_kernel, name='exchange', out_shape=(jax.ShapeDtypeStr...]
where the time goes in v2:
time: 41.5 us; the launch traced here: 41.4 us
  Pallas kernels  40.8 us (98%)
  between operations  0.64 us (2%)
    pallas_call x1, Pallas kernels, on_device(): pl.pallas_call(comm_kernel, name='exchange', out_shape=(jax.ShapeDtypeStr...  38.4 us
    pallas_call x1, Pallas kernels, on_device(): pl.pallas_call(out_kernel, name='decompress', out_shape=(jax.ShapeDtypeSt...  2.4 us

profile of v2, /device:TPU:1, one launch (start us, length us, event | category | flops | bytes accessed | tf_op | source)
XLA Modules:
  0.0 41.4 jit_solution(16431359052002680806)
XLA Ops:
  0.6 38.4 %exchange.1 = (f32[2,64,1024]{2,1,0:T(8,128)S(1)}, f32[2,64,128]{2,1,0:T(8,128)S(1)}, f32[2,64,256]{2,1,0:T(8,128)S(1)}, f32[2,256,1024]{2,1,0:T(8,128)S(1)}) custom-call(bf16[2,256,1024]{2,1,0:T(8,128)(2,1)} %bitcast.6, f32[2,256,1024]{2,1,0:T(8,128)} %bitcast.5, f32[2,64,1024]{2,1,0:T(8,128)} %bitcast.7), custom_call_target="tpu_custom_call" | custom-call | tf_op jit(solution)/shard_map/exchange/pallas_call | solution.py:306
  39.0 2.4 %decompress.1 = (bf16[2,256,1024]{2,1,0:T(8,128)(2,1)}, f32[2,256,1024]{2,1,0:T(8,128)}, f32[2,64,1024]{2,1,0:T(8,128)}) custom-call(f32[2,256,1024]{2,1,0:T(8,128)S(1)} %get-tuple-element.10.mer_ref, f32[2,64,1024]{2,1,0:T(8,128)S(1)} %get-tuple-element.11.rt_ref, f32[2,64,128]{2,1,0:T(8,128)S(1)} %get-tuple-element.12.cinv_ref, ...), custom_call_target="tpu_custom_call" | custom-call | tf_op jit(solution)/shard_map/decompress/pallas_call | solution.py:355

commit v3 on v2

--- a/solution.py
+++ b/solution.py
@@ -21,7 +21,20 @@
 NCH = 2
 CW = KVC // NCH
 PW = CW // 2
-PLANE = [(dx, dy) for dx in range(NX) for dy in range(NY) if dx or dy]
+
+
+def hops(d, n):
+    return min(d, n - d)
+
+
+PLANE = sorted(
+    ((dx, dy) for dx in range(NX) for dy in range(NY) if dx or dy),
+    key=lambda o: -hops(o[0], NX) - hops(o[1], NY),
+)
+DIST = [hops(dx, NX) + hops(dy, NY) for dx, dy in PLANE]
+ZLINE = sorted(range(1, NZ), key=lambda d: -hops(d, NZ))
+YLINE = sorted(range(1, NY), key=lambda d: -hops(d, NY))
+FAR = max(DIST)
 
 
 def split(x):
@@ -63,7 +76,7 @@
     grad_ref, err_ref, basis_ref,
     rt_out, cinv_out, ot_out, mer,
     g_o, e_o, g_s, e_s, b_v, pin, p_hi, p_lo,
-    l1, lr1, l2, lr2,
+    l1, lr,
     gz_b, gz_r, gx_b, gx_r,
     rs_b, rs_r, z_b, z_r, ag_b, w_b,
     ld, px_s, px_r, l_s, l_r, g_ss, g_rs, rs_s, rs_rs, z_s, z_rs, ag_s, ag_rs, fw_s, fw_r, co_s, co_r,
@@ -78,7 +91,8 @@
 
     partner = dev(y, z, x, 1 - c)
     plane = [(dx, dy, dev((y + dy) % NY, z, (x + dx) % NX)) for dx, dy in PLANE]
-    zline = [dev(y, (z + d) % NZ, x) for d in range(1, NZ)]
+    zline = [(d - 1, dev(y, (z + d) % NZ, x)) for d in ZLINE]
+    yline = [(d - 1, dev((y + d) % NY, z, x)) for d in YLINE]
     xline = [dev(y, z, (x + d) % NX) for d in range(1, NX)]
 
     def remote(src, dst, ss, rs, to):
@@ -147,29 +161,13 @@
     t = nt(bt2, p_hi[...])
     lt = (t[:RANK] + t[RANK:] + nt(bt_h, p_lo[...])) * 0.125
     l1[...] = lt
-    flip = y + 1 - 2 * (y % 2)
-    side = (y + 3 + 2 * (y % 2)) % NY
-    d_flip, d_side = dev(flip, z, x), dev(side, z, x)
-    half = RANK // 2
-    lo_half, hi_half = pl.ds(0, half), pl.ds(half, half)
-    a1 = remote(l1.at[lo_half], lr1.at[lo_half], l_s.at[0], l_r.at[0], d_flip)
-    b1 = remote(l1.at[hi_half], lr1.at[hi_half], l_s.at[1], l_r.at[1], d_side)
+    for d, to in yline:
+        remote(l1, lr.at[d], l_s.at[0], l_r.at[0], to)
     pl.semaphore_wait(near3, len(near))
     tell(near4, near)
-    a1.wait_recv()
-    l2[lo_half, :] = lt[:half] + lr1[lo_half, :]
-    a2 = remote(l2.at[lo_half], lr2.at[lo_half], l_s.at[2], l_r.at[2], d_side)
-    b1.wait_recv()
-    l2[hi_half, :] = lt[half:] + lr1[hi_half, :]
-    b2 = remote(l2.at[hi_half], lr2.at[hi_half], l_s.at[3], l_r.at[3], d_flip)
-    a2.wait_recv()
-    b2.wait_recv()
-    lt = l2[...] + lr2[...]
+    wait_bytes(lr, l_r.at[0])
+    lt = (lt + lr[1]) + (lr[0] + lr[2])
     pl.semaphore_wait(near4, len(near))
-
-    gram = nt(lt, lt, precision=HIGHEST)
-    gz_b[...] = jnp.concatenate([gram[: RANK // 2], gram[RANK // 2 :]], axis=1)
-    gz = [remote(gz_b, gz_r.at[d], g_ss.at[0], g_rs.at[0], to) for d, to in enumerate(zline)]
 
     lt_h, lt_l = split(lt)
     lt2 = jnp.concatenate([lt_h, lt_l], axis=0)
@@ -188,6 +186,11 @@
             rows, cols = piece(rs_b, at, j)
             remote(rs_b.at[rows, cols], rs_r.at[j, i], rs_s.at[j], rs_rs.at[j], to)
 
+    gram = nt(lt, lt, precision=HIGHEST)
+    gz_b[...] = jnp.concatenate([gram[: RANK // 2], gram[RANK // 2 :]], axis=1)
+    for d, to in zline:
+        remote(gz_b, gz_r.at[d], g_ss.at[0], g_rs.at[0], to)
+
     def gram_z():
         wait_bytes(gz_r, g_rs.at[0])
         r = [gz_b[...]] + [gz_r[d] for d in range(NZ - 1)]
@@ -202,23 +205,24 @@
         while len(r) > 1:
             r = [r[i] + r[i + 1] for i in range(0, len(r), 2)]
         z_b[j] = r[0]
-        for d, to in enumerate(zline):
+        for d, to in zline:
             remote(z_b.at[j], z_r.at[j, d], z_s.at[j], z_rs.at[j], to)
 
     def sum_z(j):
         wait_bytes(z_r.at[j], z_rs.at[j])
         r = [z_b[j]] + [z_r[j, d] for d in range(NZ - 1)]
         total = ((r[0] + r[4]) + (r[2] + r[6])) + ((r[1] + r[5]) + (r[3] + r[7]))
-        rows, cols = piece(rs_b, me, j)
         ag_b[j] = total
-        rt_out[c, rows, cols] = total
-        for _, _, to in plane:
-            remote(ag_b.at[j], rt_out.at[c, rows, cols], ag_s.at[j], ag_rs.at[j], to)
-
-    sum_rs(0)
+        rt_out[c, j, me] = total
+        for i, (_, _, to) in enumerate(plane):
+            remote(ag_b.at[j], rt_out.at[c, j, me], ag_s.at[j], ag_rs.at[j, DIST[i] - 1], to)
+        remote(ag_b.at[j], rt_out.at[c, j, me], fw_s.at[0], fw_r.at[0], partner)
+
+    for j in range(NCH):
+        sum_rs(j)
     gram_z()
-    for j in range(1, NCH):
-        sum_rs(j)
+    for j in range(NCH):
+        sum_z(j)
     wait_bytes(gx_r, g_rs.at[1])
     g = (gx_b[...] + gx_r[1]) + (gx_r[0] + gx_r[2])
     gram = jnp.concatenate([g[:, :RANK], g[:, RANK:]], axis=0)
@@ -226,10 +230,7 @@
     ci = lax.broadcasted_iota(jnp.int32, (RANK, RANK), 1)
     w = jnp.concatenate([gram, jnp.where(ri == ci, 1.0, 0.0)], axis=1)
     blocks = [w[8 * b : 8 * b + 8] for b in range(8)]
-    blocks = factor_panels(blocks, range(0, 2))
-    for j in range(NCH):
-        sum_z(j)
-    blocks = factor_panels(blocks, range(2, 8))
+    blocks = factor_panels(blocks, range(8))
     w = jnp.concatenate(blocks, axis=0)
     u, low = w[:, :RANK], w[:, RANK:]
     diag = jnp.sum(jnp.where(ri == ci, u, 0.0), axis=1, keepdims=True)
@@ -239,26 +240,26 @@
     ot_out[c] = nn(cinv, lt, precision=HIGHEST)
     remote(cinv_out.at[c], cinv_out.at[c], co_s.at[0], co_r.at[0], partner)
     remote(ot_out.at[c], ot_out.at[c], co_s.at[1], co_r.at[1], partner)
-    for j in range(NCH):
-        wait_bytes(rs_r.at[j], ag_rs.at[j])
-        cols = pl.ds(j * CW, CW)
-        remote(rt_out.at[c, :, cols], rt_out.at[c, :, cols], fw_s.at[j], fw_r.at[j], partner)
+    for j, k in sorted(((j, k) for j in range(NCH) for k in range(FAR)), key=lambda t: t[1] + 0.7 * t[0]):
+        wait_bytes(rs_r.at[j, pl.ds(0, DIST.count(k + 1))], ag_rs.at[j, k])
+        for (dx, dy, _), n in zip(plane, DIST):
+            if n == k + 1:
+                at = ((y + dy) % NY) * NX + (x + dx) % NX
+                remote(rt_out.at[c, j, at], rt_out.at[c, j, at], fw_s.at[0], fw_r.at[0], partner)
 
     wait_bytes(cinv_out.at[oc], co_r.at[0])
     wait_bytes(ot_out.at[oc], co_r.at[1])
-    for j in range(NCH):
-        wait_bytes(rt_out.at[oc, :, pl.ds(j * CW, CW)], fw_r.at[j])
+    wait_bytes(rt_out.at[oc], fw_r.at[0])
     for q in range(NQ):
         px[q].wait_send()
-    for cp in (a1, b1, a2, b2):
-        cp.wait_send()
+    wait_bytes(lr, l_s.at[0])
     wait_bytes(gz_r, g_ss.at[0])
     wait_bytes(gx_r, g_ss.at[1])
     for j in range(NCH):
         wait_bytes(rs_r.at[j], rs_s.at[j])
         wait_bytes(z_r.at[j], z_s.at[j])
         wait_bytes(rs_r.at[j], ag_s.at[j])
-        wait_bytes(rt_out.at[c, :, pl.ds(j * CW, CW)], fw_s.at[j])
+    wait_bytes(rt_out.at[c], fw_s.at[0])
     wait_bytes(cinv_out.at[c], co_s.at[0])
     wait_bytes(ot_out.at[c], co_s.at[1])
 
@@ -276,7 +277,14 @@
 
     for m in range(2):
         ch, cl = split(cinv_ref[m][:, :RANK] * 0.125)
-        rh, rl = split(rt_ref[m])
+        raw = jnp.concatenate(
+            [
+                jnp.concatenate([rt_ref[m, j, 2 * k + h] for j in range(NCH) for h in range(2)], axis=1)
+                for k in range(RANK // 8)
+            ],
+            axis=0,
+        )
+        rh, rl = split(raw)
         right = nn(jnp.concatenate([ch, cl], axis=1), jnp.concatenate([rh, rh], axis=0)) + nn(ch, rl)
         nxt[m] = right
         out(nxt.at[m], next_ref.at[m], sems.at[0, m])
@@ -307,7 +315,7 @@
         comm_kernel,
         name="exchange",
         out_shape=(
-            jax.ShapeDtypeStruct((2, RANK, KVC), F32),
+            jax.ShapeDtypeStruct((2, NCH, NX * NY, 8, PW), F32),
             jax.ShapeDtypeStruct((2, RANK, 128), F32),
             jax.ShapeDtypeStruct((2, RANK, ROWS), F32),
             jax.ShapeDtypeStruct((2, ROWS, KVC), F32),
@@ -324,9 +332,7 @@
             pltpu.VMEM((ROWS, KVC), BF16),
             pltpu.VMEM((ROWS, KVC), BF16),
             pltpu.VMEM((RANK, ROWS), F32),
-            pltpu.VMEM((RANK, ROWS), F32),
-            pltpu.VMEM((RANK, ROWS), F32),
-            pltpu.VMEM((RANK, ROWS), F32),
+            pltpu.VMEM((NY - 1, RANK, ROWS), F32),
             pltpu.VMEM((RANK // 2, 128), F32),
             pltpu.VMEM((NZ - 1, RANK // 2, 128), F32),
             pltpu.VMEM((RANK // 2, 128), F32),
@@ -340,12 +346,13 @@
             dma((2 * NQ + 3,)),
             dma((NQ,)),
             dma((NQ,)),
-            dma((4,)),
-            dma((4,)),
+            dma((1,)),
+            dma((1,)),
             dma((2,)),
             dma((2,)),
         ]
-        + [dma((NCH,))] * 8
+        + [dma((NCH,))] * 5
+        + [dma((NCH, FAR)), dma((1,)), dma((1,))]
         + [dma((2,)), dma((2,))]
         + [pltpu.SemaphoreType.REGULAR] * 3,
         compiler_params=pltpu.CompilerParams(

time: 41.5 us -> 38.6 us (0.930)
  Pallas kernels: 40.8 us -> 37.9 us
    pallas_call x1, Pallas kernels: 38.4 us -> 35.5 us  [on_device(): pl.pallas_call(comm_kernel, name='exchange', out_shape=(jax.ShapeDtypeStr...]
where the time goes in v3:
time: 38.6 us; the launch traced here: 38.5 us
  Pallas kernels  37.9 us (98%)
  between operations  0.64 us (2%)
    pallas_call x1, Pallas kernels, on_device(): pl.pallas_call(comm_kernel, name='exchange', out_shape=(jax.ShapeDtypeStr...  35.5 us
    pallas_call x1, Pallas kernels, on_device(): pl.pallas_call(out_kernel, name='decompress', out_shape=(jax.ShapeDtypeSt...  2.4 us

profile of v3, /device:TPU:1, one launch (start us, length us, event | category | flops | bytes accessed | tf_op | source)
XLA Modules:
  0.0 38.5 jit_solution(17720003591451709556)
XLA Ops:
  0.6 35.5 %exchange.1 = (f32[2,2,16,8,256]{4,3,2,1,0:T(8,128)S(1)}, f32[2,64,128]{2,1,0:T(8,128)S(1)}, f32[2,64,256]{2,1,0:T(8,128)S(1)}, f32[2,256,1024]{2,1,0:T(8,128)S(1)}) custom-call(bf16[2,256,1024]{2,1,0:T(8,128)(2,1)} %bitcast.6, f32[2,256,1024]{2,1,0:T(8,128)} %bitcast.5, f32[2,64,1024]{2,1,0:T(8,128)} %bitcast.7), custom_call_target="tpu_custom_call" | custom-call | tf_op jit(solution)/shard_map/exchange/pallas_call | solution.py:314
  36.1 2.4 %decompress.1 = (bf16[2,256,1024]{2,1,0:T(8,128)(2,1)}, f32[2,256,1024]{2,1,0:T(8,128)}, f32[2,64,1024]{2,1,0:T(8,128)}) custom-call(f32[2,256,1024]{2,1,0:T(8,128)S(1)} %get-tuple-element.10.mer_ref, f32[2,2,16,8,256]{4,3,2,1,0:T(8,128)S(1)} %get-tuple-element.11.rt_ref, f32[2,64,128]{2,1,0:T(8,128)S(1)} %get-tuple-element.12.cinv_ref, ...), custom_call_target="tpu_custom_call" | custom-call | tf_op jit(solution)/shard_map/decompress/pallas_call | solution.py:362

commit v4 on v3

--- a/solution.py
+++ b/solution.py
@@ -16,11 +16,12 @@
 KVC = 1024
 RANK = 64
 NX, NY, NZ = 4, 4, 8
-NQ = 4
+NQ = 2
 QR = ROWS // NQ
-NCH = 2
-CW = KVC // NCH
-PW = CW // 2
+NCH = 4
+KR = RANK // NCH
+CPR = NX * NY * 8 // KR
+PW = KVC // CPR
 
 
 def hops(d, n):
@@ -35,6 +36,7 @@
 ZLINE = sorted(range(1, NZ), key=lambda d: -hops(d, NZ))
 YLINE = sorted(range(1, NY), key=lambda d: -hops(d, NY))
 FAR = max(DIST)
+NP = len(PLANE)
 
 
 def split(x):
@@ -80,7 +82,7 @@
     gz_b, gz_r, gx_b, gx_r,
     rs_b, rs_r, z_b, z_r, ag_b, w_b,
     ld, px_s, px_r, l_s, l_r, g_ss, g_rs, rs_s, rs_rs, z_s, z_rs, ag_s, ag_rs, fw_s, fw_r, co_s, co_r,
-    near2, near3, near4,
+    near2, near3, near4, near5,
 ):
     rep, shard = lax.axis_index("rep"), lax.axis_index("shard")
     y, c = rep // 2, rep % 2
@@ -90,7 +92,7 @@
         return (yy * 2 + (c if cc is None else cc), zz * NX + xx)
 
     partner = dev(y, z, x, 1 - c)
-    plane = [(dx, dy, dev((y + dy) % NY, z, (x + dx) % NX)) for dx, dy in PLANE]
+    plane = [(dx, dy, dev((y + dy) % NY, z, (x + dx) % NX, 1)) for dx, dy in PLANE]
     zline = [(d - 1, dev(y, (z + d) % NZ, x)) for d in ZLINE]
     yline = [(d - 1, dev((y + d) % NY, z, x)) for d in YLINE]
     xline = [dev(y, z, (x + d) % NX) for d in range(1, NX)]
@@ -158,34 +160,46 @@
         h, l = split(mer[c, rows, :] + pin[rows, :])
         p_hi[rows, :] = h
         p_lo[rows, :] = l
+    pl.semaphore_wait(near3, len(near))
+    tell(near4, near)
     t = nt(bt2, p_hi[...])
     lt = (t[:RANK] + t[RANK:] + nt(bt_h, p_lo[...])) * 0.125
     l1[...] = lt
-    for d, to in yline:
-        remote(l1, lr.at[d], l_s.at[0], l_r.at[0], to)
-    pl.semaphore_wait(near3, len(near))
-    tell(near4, near)
-    wait_bytes(lr, l_r.at[0])
-    lt = (lt + lr[1]) + (lr[0] + lr[2])
+    for j in range(NCH):
+        rows = pl.ds(j * KR, KR)
+        for d, to in yline:
+            remote(l1.at[rows], lr.at[d, rows], l_s.at[j], l_r.at[j], to)
     pl.semaphore_wait(near4, len(near))
-
-    lt_h, lt_l = split(lt)
-    lt2 = jnp.concatenate([lt_h, lt_l], axis=0)
-
-    def piece(ref, p, j):
-        rows = pl.ds(pl.multiple_of((p // 2) * 8, 8), 8)
-        cols = pl.ds(pl.multiple_of(j * CW + (p % 2) * PW, PW), PW)
+    tell(near5, near)
+
+    def piece(p, j):
+        rows = pl.ds(pl.multiple_of(j * KR + (p // CPR) * 8, 8), 8)
+        cols = pl.ds(pl.multiple_of((p % CPR) * PW, PW), PW)
         return rows, cols
 
     me = y * NX + x
+    ltj = []
     for j in range(NCH):
-        t = nn(lt2, p_hi[:, j * CW : (j + 1) * CW])
-        rs_b[:, j * CW : (j + 1) * CW] = t[:RANK] + t[RANK:] + nn(lt_h, p_lo[:, j * CW : (j + 1) * CW])
+        rows = slice(j * KR, (j + 1) * KR)
+        wait_bytes(lr.at[:, pl.ds(j * KR, KR)], l_r.at[j])
+        part = (lt[rows] + lr[1, rows]) + (lr[0, rows] + lr[2, rows])
+        ltj.append(part)
+        h, l = split(part)
+        t = nn(jnp.concatenate([h, l], axis=0), p_hi[...])
+        rs_b[rows, :] = t[:KR] + t[KR:] + nn(h, p_lo[...])
+        if j == 0:
+            pl.semaphore_wait(near5, len(near))
         for i, (dx, dy, to) in enumerate(plane):
             at = ((y + dy) % NY) * NX + (x + dx) % NX
-            rows, cols = piece(rs_b, at, j)
-            remote(rs_b.at[rows, cols], rs_r.at[j, i], rs_s.at[j], rs_rs.at[j], to)
-
+            rows, cols = piece(at, j)
+            remote(rs_b.at[rows, cols], rs_r.at[c, j, i], rs_s.at[j], rs_rs.at[c, j], to)
+
+        @pl.when(c == 0)
+        def _():
+            rows, cols = piece(me, j)
+            remote(rs_b.at[rows, cols], rs_r.at[0, j, NP], rs_s.at[j], rs_rs.at[0, j], partner)
+
+    lt = jnp.concatenate(ltj, axis=0)
     gram = nt(lt, lt, precision=HIGHEST)
     gz_b[...] = jnp.concatenate([gram[: RANK // 2], gram[RANK // 2 :]], axis=1)
     for d, to in zline:
@@ -198,31 +212,50 @@
         for d, to in enumerate(xline):
             remote(gx_b, gx_r.at[d], g_ss.at[1], g_rs.at[1], to)
 
-    def sum_rs(j):
-        wait_bytes(rs_r.at[j], rs_rs.at[j])
-        rows, cols = piece(rs_b, me, j)
-        r = [rs_b[rows, cols]] + [rs_r[j, i] for i in range(len(PLANE))]
+    def tree(r):
         while len(r) > 1:
             r = [r[i] + r[i + 1] for i in range(0, len(r), 2)]
-        z_b[j] = r[0]
-        for d, to in zline:
-            remote(z_b.at[j], z_r.at[j, d], z_s.at[j], z_rs.at[j], to)
-
-    def sum_z(j):
-        wait_bytes(z_r.at[j], z_rs.at[j])
-        r = [z_b[j]] + [z_r[j, d] for d in range(NZ - 1)]
+        return r[0]
+
+    @pl.when(c == 1)
+    def _():
+        for m in (1, 0):
+            for j in range(NCH):
+                if m == 1:
+                    wait_bytes(rs_r.at[m, j, pl.ds(0, NP)], rs_rs.at[m, j])
+                    rows, cols = piece(me, j)
+                    last = rs_b[rows, cols]
+                else:
+                    wait_bytes(rs_r.at[m, j], rs_rs.at[m, j])
+                    last = rs_r[m, j, NP]
+                total = tree([rs_r[m, j, i] for i in range(NP)] + [last])
+                z_b[m, j] = total
+                for d in ZLINE:
+                    remote(z_b.at[m, j], z_r.at[j, d], z_s.at[m, j], z_rs.at[j], dev(y, (z + d) % NZ, x, m))
+                if m == 1:
+                    z_r[j, 0] = total
+                else:
+                    remote(z_b.at[m, j], z_r.at[j, 0], z_s.at[m, j], z_rs.at[j], partner)
+
+    gram_z()
+    for j in range(NCH):
+
+        @pl.when(c == 1)
+        def _():
+            wait_bytes(z_r.at[j, pl.ds(1, NZ - 1)], z_rs.at[j])
+
+        @pl.when(c == 0)
+        def _():
+            wait_bytes(z_r.at[j], z_rs.at[j])
+
+        r = [z_r[j, d] for d in range(NZ)]
         total = ((r[0] + r[4]) + (r[2] + r[6])) + ((r[1] + r[5]) + (r[3] + r[7]))
         ag_b[j] = total
         rt_out[c, j, me] = total
         for i, (_, _, to) in enumerate(plane):
-            remote(ag_b.at[j], rt_out.at[c, j, me], ag_s.at[j], ag_rs.at[j, DIST[i] - 1], to)
+            remote(ag_b.at[j], rt_out.at[c, j, me], ag_s.at[j], ag_rs.at[c, j, DIST[i] - 1], to)
         remote(ag_b.at[j], rt_out.at[c, j, me], fw_s.at[0], fw_r.at[0], partner)
 
-    for j in range(NCH):
-        sum_rs(j)
-    gram_z()
-    for j in range(NCH):
-        sum_z(j)
     wait_bytes(gx_r, g_rs.at[1])
     g = (gx_b[...] + gx_r[1]) + (gx_r[0] + gx_r[2])
     gram = jnp.concatenate([g[:, :RANK], g[:, RANK:]], axis=0)
@@ -240,26 +273,43 @@
     ot_out[c] = nn(cinv, lt, precision=HIGHEST)
     remote(cinv_out.at[c], cinv_out.at[c], co_s.at[0], co_r.at[0], partner)
     remote(ot_out.at[c], ot_out.at[c], co_s.at[1], co_r.at[1], partner)
-    for j, k in sorted(((j, k) for j in range(NCH) for k in range(FAR)), key=lambda t: t[1] + 0.7 * t[0]):
-        wait_bytes(rs_r.at[j, pl.ds(0, DIST.count(k + 1))], ag_rs.at[j, k])
-        for (dx, dy, _), n in zip(plane, DIST):
-            if n == k + 1:
-                at = ((y + dy) % NY) * NX + (x + dx) % NX
-                remote(rt_out.at[c, j, at], rt_out.at[c, j, at], fw_s.at[0], fw_r.at[0], partner)
-
+    @pl.when(c == 1)
+    def _():
+        order = sorted(
+            ((m, j, k) for m in range(2) for j in range(NCH) for k in range(FAR)),
+            key=lambda t: t[2] * 0.6 + 0.5 * t[1] - t[0],
+        )
+        for m, j, k in order:
+            wait_bytes(rs_r.at[m, j, pl.ds(0, DIST.count(k + 1))], ag_rs.at[m, j, k])
+            for (dx, dy), n in zip(PLANE, DIST):
+                if n == k + 1:
+                    at = ((y + dy) % NY) * NX + (x + dx) % NX
+                    remote(rt_out.at[m, j, at], rt_out.at[m, j, at], fw_s.at[1], fw_r.at[1], partner)
+        wait_bytes(rt_out.at[:, :, pl.ds(0, NP)], fw_s.at[1])
+        for m in range(2):
+            for j in range(NCH):
+                wait_bytes(z_r.at[j, pl.ds(0, NZ - m)], z_s.at[m, j])
+                wait_bytes(rs_r.at[1, j, pl.ds(0, NP)], rs_s.at[j]) if m else None
+
+    @pl.when(c == 0)
+    def _():
+        wait_bytes(rt_out.at[:, :, pl.ds(0, NP)], fw_r.at[1])
+        for j in range(NCH):
+            wait_bytes(rs_r.at[0, j], rs_s.at[j])
+
+    own = rt_out.at[0, :, 0]
+    wait_bytes(own, fw_r.at[0])
+    wait_bytes(own, fw_s.at[0])
     wait_bytes(cinv_out.at[oc], co_r.at[0])
     wait_bytes(ot_out.at[oc], co_r.at[1])
-    wait_bytes(rt_out.at[oc], fw_r.at[0])
     for q in range(NQ):
         px[q].wait_send()
-    wait_bytes(lr, l_s.at[0])
+    for j in range(NCH):
+        wait_bytes(lr.at[:, pl.ds(j * KR, KR)], l_s.at[j])
     wait_bytes(gz_r, g_ss.at[0])
     wait_bytes(gx_r, g_ss.at[1])
     for j in range(NCH):
-        wait_bytes(rs_r.at[j], rs_s.at[j])
-        wait_bytes(z_r.at[j], z_s.at[j])
-        wait_bytes(rs_r.at[j], ag_s.at[j])
-    wait_bytes(rt_out.at[c], fw_s.at[0])
+        wait_bytes(rs_r.at[0, j, pl.ds(0, NP)], ag_s.at[j])
     wait_bytes(cinv_out.at[c], co_s.at[0])
     wait_bytes(ot_out.at[c], co_s.at[1])
 
@@ -279,8 +329,9 @@
         ch, cl = split(cinv_ref[m][:, :RANK] * 0.125)
         raw = jnp.concatenate(
             [
-                jnp.concatenate([rt_ref[m, j, 2 * k + h] for j in range(NCH) for h in range(2)], axis=1)
-                for k in range(RANK // 8)
+                jnp.concatenate([rt_ref[m, j, g * CPR + h] for h in range(CPR)], axis=1)
+                for j in range(NCH)
+                for g in range(KR // 8)
             ],
             axis=0,
         )
@@ -338,23 +389,22 @@
             pltpu.VMEM((RANK // 2, 128), F32),
             pltpu.VMEM((NX - 1, RANK // 2, 128), F32),
             pltpu.VMEM((RANK, KVC), F32),
-            pltpu.VMEM((NCH, len(PLANE), 8, PW), F32),
-            pltpu.VMEM((NCH, 8, PW), F32),
-            pltpu.VMEM((NCH, NZ - 1, 8, PW), F32),
+            pltpu.VMEM((2, NCH, NP + 1, 8, PW), F32),
+            pltpu.VMEM((2, NCH, 8, PW), F32),
+            pltpu.VMEM((NCH, NZ, 8, PW), F32),
             pltpu.VMEM((NCH, 8, PW), F32),
             pltpu.VMEM((RANK, 128), F32),
             dma((2 * NQ + 3,)),
             dma((NQ,)),
             dma((NQ,)),
-            dma((1,)),
-            dma((1,)),
+            dma((NCH,)),
+            dma((NCH,)),
             dma((2,)),
             dma((2,)),
         ]
-        + [dma((NCH,))] * 5
-        + [dma((NCH, FAR)), dma((1,)), dma((1,))]
+        + [dma((NCH,)), dma((2, NCH)), dma((2, NCH)), dma((NCH,)), dma((NCH,)), dma((2, NCH, FAR)), dma((2,)), dma((2,))]
         + [dma((2,)), dma((2,))]
-        + [pltpu.SemaphoreType.REGULAR] * 3,
+        + [pltpu.SemaphoreType.REGULAR] * 4,
         compiler_params=pltpu.CompilerParams(
             collective_id=0, has_side_effects=True, vmem_limit_bytes=40 << 20
         ),

time: 38.6 us -> 36.8 us (0.953)
  Pallas kernels: 37.9 us -> 36.1 us
    pallas_call x1, Pallas kernels: 35.5 us -> 33.7 us  [on_device(): pl.pallas_call(comm_kernel, name='exchange', out_shape=(jax.ShapeDtypeStr...]
where the time goes in v4:
time: 36.8 us; the launch traced here: 36.7 us
  Pallas kernels  36.1 us (98%)
  between operations  0.64 us (2%)
    pallas_call x1, Pallas kernels, on_device(): pl.pallas_call(comm_kernel, name='exchange', out_shape=(jax.ShapeDtypeStr...  33.7 us
    pallas_call x1, Pallas kernels, on_device(): pl.pallas_call(out_kernel, name='decompress', out_shape=(jax.ShapeDtypeSt...  2.4 us

profile of v4, /device:TPU:1, one launch (start us, length us, event | category | flops | bytes accessed | tf_op | source)
XLA Modules:
  0.0 36.7 jit_solution(8184017342668967751)
XLA Ops:
  0.6 33.7 %exchange.1 = (f32[2,4,16,8,128]{4,3,2,1,0:T(8,128)S(1)}, f32[2,64,128]{2,1,0:T(8,128)S(1)}, f32[2,64,256]{2,1,0:T(8,128)S(1)}, f32[2,256,1024]{2,1,0:T(8,128)S(1)}) custom-call(bf16[2,256,1024]{2,1,0:T(8,128)(2,1)} %bitcast.6, f32[2,256,1024]{2,1,0:T(8,128)} %bitcast.5, f32[2,64,1024]{2,1,0:T(8,128)} %bitcast.7), custom_call_target="tpu_custom_call" | custom-call | tf_op jit(solution)/shard_map/exchange/pallas_call | solution.py:365
  34.3 2.4 %decompress.1 = (bf16[2,256,1024]{2,1,0:T(8,128)(2,1)}, f32[2,256,1024]{2,1,0:T(8,128)}, f32[2,64,1024]{2,1,0:T(8,128)}) custom-call(f32[2,256,1024]{2,1,0:T(8,128)S(1)} %get-tuple-element.10.mer_ref, f32[2,4,16,8,128]{4,3,2,1,0:T(8,128)S(1)} %get-tuple-element.11.rt_ref, f32[2,64,128]{2,1,0:T(8,128)S(1)} %get-tuple-element.12.cinv_ref, ...), custom_call_target="tpu_custom_call" | custom-call | tf_op jit(solution)/shard_map/decompress/pallas_call | solution.py:412

commit v5 on v4

--- a/solution.py
+++ b/solution.py
@@ -18,7 +18,7 @@
 NX, NY, NZ = 4, 4, 8
 NQ = 2
 QR = ROWS // NQ
-NCH = 4
+NCH = 2
 KR = RANK // NCH
 CPR = NX * NY * 8 // KR
 PW = KVC // CPR
@@ -37,6 +37,7 @@
 YLINE = sorted(range(1, NY), key=lambda d: -hops(d, NY))
 FAR = max(DIST)
 NP = len(PLANE)
+NF = NP - DIST.count(FAR)
 
 
 def split(x):
@@ -81,7 +82,7 @@
     l1, lr,
     gz_b, gz_r, gx_b, gx_r,
     rs_b, rs_r, z_b, z_r, ag_b, w_b,
-    ld, px_s, px_r, l_s, l_r, g_ss, g_rs, rs_s, rs_rs, z_s, z_rs, ag_s, ag_rs, fw_s, fw_r, co_s, co_r,
+    ld, px_s, px_r, l_s, l_r, g_ss, g_rs, rs_s, rs_rs, z_s, z_rs, ag_s, ag_rs, fw_s, fw_r, dr_s, dr_r, co_s, co_r,
     near2, near3, near4, near5,
 ):
     rep, shard = lax.axis_index("rep"), lax.axis_index("shard")
@@ -154,23 +155,27 @@
     mer[c] = g_s[...].astype(F32) + e_s[...]
     pl.semaphore_wait(near2, len(near))
     tell(near3, near)
+    lq = []
     for q in range(NQ):
         rows = pl.ds(q * QR, QR)
         px[q].wait_recv()
         h, l = split(mer[c, rows, :] + pin[rows, :])
         p_hi[rows, :] = h
         p_lo[rows, :] = l
-    pl.semaphore_wait(near3, len(near))
-    tell(near4, near)
-    t = nt(bt2, p_hi[...])
-    lt = (t[:RANK] + t[RANK:] + nt(bt_h, p_lo[...])) * 0.125
-    l1[...] = lt
-    for j in range(NCH):
-        rows = pl.ds(j * KR, KR)
+        t = nt(bt2, h)
+        lq.append((t[:RANK] + t[RANK:] + nt(bt_h, l)) * 0.125)
+        l1[q] = lq[q]
         for d, to in yline:
-            remote(l1.at[rows], lr.at[d, rows], l_s.at[j], l_r.at[j], to)
+            remote(l1.at[q], lr.at[d, q], l_s.at[q], l_r.at[q], to)
+        if q == 0:
+            pl.semaphore_wait(near3, len(near))
+            tell(near4, near)
     pl.semaphore_wait(near4, len(near))
     tell(near5, near)
+    for q in range(NQ):
+        wait_bytes(lr.at[:, q], l_r.at[q])
+        lq[q] = (lq[q] + lr[1, q]) + (lr[0, q] + lr[2, q])
+    lt = jnp.concatenate(lq, axis=1)
 
     def piece(p, j):
         rows = pl.ds(pl.multiple_of(j * KR + (p // CPR) * 8, 8), 8)
@@ -178,12 +183,9 @@
         return rows, cols
 
     me = y * NX + x
-    ltj = []
     for j in range(NCH):
         rows = slice(j * KR, (j + 1) * KR)
-        wait_bytes(lr.at[:, pl.ds(j * KR, KR)], l_r.at[j])
-        part = (lt[rows] + lr[1, rows]) + (lr[0, rows] + lr[2, rows])
-        ltj.append(part)
+        part = lt[rows]
         h, l = split(part)
         t = nn(jnp.concatenate([h, l], axis=0), p_hi[...])
         rs_b[rows, :] = t[:KR] + t[KR:] + nn(h, p_lo[...])
@@ -199,7 +201,6 @@
             rows, cols = piece(me, j)
             remote(rs_b.at[rows, cols], rs_r.at[0, j, NP], rs_s.at[j], rs_rs.at[0, j], partner)
 
-    lt = jnp.concatenate(ltj, axis=0)
     gram = nt(lt, lt, precision=HIGHEST)
     gz_b[...] = jnp.concatenate([gram[: RANK // 2], gram[RANK // 2 :]], axis=1)
     for d, to in zline:
@@ -231,8 +232,8 @@
                 total = tree([rs_r[m, j, i] for i in range(NP)] + [last])
                 z_b[m, j] = total
                 for d in ZLINE:
-                    remote(z_b.at[m, j], z_r.at[j, d], z_s.at[m, j], z_rs.at[j], dev(y, (z + d) % NZ, x, m))
-                if m == 1:
+                    remote(z_b.at[m, j], z_r.at[j, d], z_s.at[m, j], z_rs.at[j], dev(y, (z + d) % NZ, x, 1 - m))
+                if m == 0:
                     z_r[j, 0] = total
                 else:
                     remote(z_b.at[m, j], z_r.at[j, 0], z_s.at[m, j], z_rs.at[j], partner)
@@ -251,10 +252,13 @@
         r = [z_r[j, d] for d in range(NZ)]
         total = ((r[0] + r[4]) + (r[2] + r[6])) + ((r[1] + r[5]) + (r[3] + r[7]))
         ag_b[j] = total
-        rt_out[c, j, me] = total
-        for i, (_, _, to) in enumerate(plane):
-            remote(ag_b.at[j], rt_out.at[c, j, me], ag_s.at[j], ag_rs.at[c, j, DIST[i] - 1], to)
-        remote(ag_b.at[j], rt_out.at[c, j, me], fw_s.at[0], fw_r.at[0], partner)
+        rt_out[oc, j, me] = total
+        for i, (dx, dy, to) in enumerate(plane):
+            if DIST[i] == FAR:
+                both = dev((y + dy) % NY, z, (x + dx) % NX, 0)
+                remote(ag_b.at[j], rt_out.at[oc, j, me], dr_s.at[0], dr_r.at[0], both)
+            remote(ag_b.at[j], rt_out.at[oc, j, me], ag_s.at[j], ag_rs.at[oc, j, DIST[i] - 1], to)
+        remote(ag_b.at[j], rt_out.at[oc, j, me], fw_s.at[0], fw_r.at[0], partner)
 
     wait_bytes(gx_r, g_rs.at[1])
     g = (gx_b[...] + gx_r[1]) + (gx_r[0] + gx_r[2])
@@ -277,35 +281,37 @@
     def _():
         order = sorted(
             ((m, j, k) for m in range(2) for j in range(NCH) for k in range(FAR)),
-            key=lambda t: t[2] * 0.6 + 0.5 * t[1] - t[0],
+            key=lambda t: t[2] * 0.6 + 0.3 * t[1] - 0.4 * t[0],
         )
         for m, j, k in order:
             wait_bytes(rs_r.at[m, j, pl.ds(0, DIST.count(k + 1))], ag_rs.at[m, j, k])
             for (dx, dy), n in zip(PLANE, DIST):
-                if n == k + 1:
+                if n == k + 1 < FAR:
                     at = ((y + dy) % NY) * NX + (x + dx) % NX
                     remote(rt_out.at[m, j, at], rt_out.at[m, j, at], fw_s.at[1], fw_r.at[1], partner)
-        wait_bytes(rt_out.at[:, :, pl.ds(0, NP)], fw_s.at[1])
+        wait_bytes(rt_out.at[:, :, pl.ds(0, NF)], fw_s.at[1])
         for m in range(2):
             for j in range(NCH):
-                wait_bytes(z_r.at[j, pl.ds(0, NZ - m)], z_s.at[m, j])
+                wait_bytes(z_r.at[j, pl.ds(0, NZ - 1 + m)], z_s.at[m, j])
                 wait_bytes(rs_r.at[1, j, pl.ds(0, NP)], rs_s.at[j]) if m else None
 
     @pl.when(c == 0)
     def _():
-        wait_bytes(rt_out.at[:, :, pl.ds(0, NP)], fw_r.at[1])
+        wait_bytes(rt_out.at[:, :, pl.ds(0, NF)], fw_r.at[1])
+        wait_bytes(rt_out.at[:, :, pl.ds(0, NP - NF)], dr_r.at[0])
         for j in range(NCH):
             wait_bytes(rs_r.at[0, j], rs_s.at[j])
 
     own = rt_out.at[0, :, 0]
     wait_bytes(own, fw_r.at[0])
     wait_bytes(own, fw_s.at[0])
+    wait_bytes(rt_out.at[0, :, pl.ds(0, NP - NF)], dr_s.at[0])
     wait_bytes(cinv_out.at[oc], co_r.at[0])
     wait_bytes(ot_out.at[oc], co_r.at[1])
     for q in range(NQ):
         px[q].wait_send()
-    for j in range(NCH):
-        wait_bytes(lr.at[:, pl.ds(j * KR, KR)], l_s.at[j])
+    for q in range(NQ):
+        wait_bytes(lr.at[:, q], l_s.at[q])
     wait_bytes(gz_r, g_ss.at[0])
     wait_bytes(gx_r, g_ss.at[1])
     for j in range(NCH):
@@ -345,6 +351,7 @@
         r3[m, 2 * RANK :] = l
         oh, ol = split(ot_ref[m].T)
         o3[m] = jnp.concatenate([oh, ol, oh], axis=1)
+    for m in range(2):
         for i in range(ROWS // OB):
             rows = pl.ds(i * OB, OB)
             approx = nn(o3[m, rows, :], r3[m])
@@ -382,8 +389,8 @@
             pltpu.VMEM((ROWS, KVC), F32),
             pltpu.VMEM((ROWS, KVC), BF16),
             pltpu.VMEM((ROWS, KVC), BF16),
-            pltpu.VMEM((RANK, ROWS), F32),
-            pltpu.VMEM((NY - 1, RANK, ROWS), F32),
+            pltpu.VMEM((NQ, RANK, QR), F32),
+            pltpu.VMEM((NY - 1, NQ, RANK, QR), F32),
             pltpu.VMEM((RANK // 2, 128), F32),
             pltpu.VMEM((NZ - 1, RANK // 2, 128), F32),
             pltpu.VMEM((RANK // 2, 128), F32),
@@ -397,12 +404,12 @@
             dma((2 * NQ + 3,)),
             dma((NQ,)),
             dma((NQ,)),
-            dma((NCH,)),
-            dma((NCH,)),
+            dma((NQ,)),
+            dma((NQ,)),
             dma((2,)),
             dma((2,)),
         ]
-        + [dma((NCH,)), dma((2, NCH)), dma((2, NCH)), dma((NCH,)), dma((NCH,)), dma((2, NCH, FAR)), dma((2,)), dma((2,))]
+        + [dma((NCH,)), dma((2, NCH)), dma((2, NCH)), dma((NCH,)), dma((NCH,)), dma((2, NCH, FAR)), dma((2,)), dma((2,)), dma((1,)), dma((1,))]
         + [dma((2,)), dma((2,))]
         + [pltpu.SemaphoreType.REGULAR] * 4,
         compiler_params=pltpu.CompilerParams(

time: 36.8 us -> 36.1 us (0.981)
  Pallas kernels: 36.1 us -> 35.4 us
    pallas_call x1, Pallas kernels: 33.7 us -> 33 us  [on_device(): pl.pallas_call(comm_kernel, name='exchange', out_shape=(jax.ShapeDtypeStr...]
where the time goes in v5:
time: 36.1 us; the launch traced here: 36 us
  Pallas kernels  35.4 us (98%)
  between operations  0.64 us (2%)
    pallas_call x1, Pallas kernels, on_device(): pl.pallas_call(comm_kernel, name='exchange', out_shape=(jax.ShapeDtypeStr...  33 us
    pallas_call x1, Pallas kernels, on_device(): pl.pallas_call(out_kernel, name='decompress', out_shape=(jax.ShapeDtypeSt...  2.33 us

profile of v5, /device:TPU:1, one launch (start us, length us, event | category | flops | bytes accessed | tf_op | source)
XLA Modules:
  0.0 36.0 jit_solution(3964492013065109186)
XLA Ops:
  0.6 33.0 %exchange.1 = (f32[2,2,16,8,256]{4,3,2,1,0:T(8,128)S(1)}, f32[2,64,128]{2,1,0:T(8,128)S(1)}, f32[2,64,256]{2,1,0:T(8,128)S(1)}, f32[2,256,1024]{2,1,0:T(8,128)S(1)}) custom-call(bf16[2,256,1024]{2,1,0:T(8,128)(2,1)} %bitcast.6, f32[2,256,1024]{2,1,0:T(8,128)} %bitcast.5, f32[2,64,1024]{2,1,0:T(8,128)} %bitcast.7), custom_call_target="tpu_custom_call" | custom-call | tf_op jit(solution)/shard_map/exchange/pallas_call | solution.py:372
  33.7 2.3 %decompress.1 = (bf16[2,256,1024]{2,1,0:T(8,128)(2,1)}, f32[2,256,1024]{2,1,0:T(8,128)}, f32[2,64,1024]{2,1,0:T(8,128)}) custom-call(f32[2,256,1024]{2,1,0:T(8,128)S(1)} %get-tuple-element.10.mer_ref, f32[2,2,16,8,256]{4,3,2,1,0:T(8,128)S(1)} %get-tuple-element.11.rt_ref, f32[2,64,128]{2,1,0:T(8,128)S(1)} %get-tuple-element.12.cinv_ref, ...), custom_call_target="tpu_custom_call" | custom-call | tf_op jit(solution)/shard_map/decompress/pallas_call | solution.py:419

commit v6 on v5

--- a/solution.py
+++ b/solution.py
@@ -37,7 +37,6 @@
 YLINE = sorted(range(1, NY), key=lambda d: -hops(d, NY))
 FAR = max(DIST)
 NP = len(PLANE)
-NF = NP - DIST.count(FAR)
 
 
 def split(x):
@@ -82,7 +81,7 @@
     l1, lr,
     gz_b, gz_r, gx_b, gx_r,
     rs_b, rs_r, z_b, z_r, ag_b, w_b,
-    ld, px_s, px_r, l_s, l_r, g_ss, g_rs, rs_s, rs_rs, z_s, z_rs, ag_s, ag_rs, fw_s, fw_r, dr_s, dr_r, co_s, co_r,
+    ld, px_s, px_r, l_s, l_r, g_ss, g_rs, rs_s, rs_rs, z_s, z_rs, ag_s, ag_rs, fw_s, fw_r, co_s, co_r,
     near2, near3, near4, near5,
 ):
     rep, shard = lax.axis_index("rep"), lax.axis_index("shard")
@@ -254,9 +253,6 @@
         ag_b[j] = total
         rt_out[oc, j, me] = total
         for i, (dx, dy, to) in enumerate(plane):
-            if DIST[i] == FAR:
-                both = dev((y + dy) % NY, z, (x + dx) % NX, 0)
-                remote(ag_b.at[j], rt_out.at[oc, j, me], dr_s.at[0], dr_r.at[0], both)
             remote(ag_b.at[j], rt_out.at[oc, j, me], ag_s.at[j], ag_rs.at[oc, j, DIST[i] - 1], to)
         remote(ag_b.at[j], rt_out.at[oc, j, me], fw_s.at[0], fw_r.at[0], partner)
 
@@ -286,10 +282,10 @@
         for m, j, k in order:
             wait_bytes(rs_r.at[m, j, pl.ds(0, DIST.count(k + 1))], ag_rs.at[m, j, k])
             for (dx, dy), n in zip(PLANE, DIST):
-                if n == k + 1 < FAR:
+                if n == k + 1:
                     at = ((y + dy) % NY) * NX + (x + dx) % NX
                     remote(rt_out.at[m, j, at], rt_out.at[m, j, at], fw_s.at[1], fw_r.at[1], partner)
-        wait_bytes(rt_out.at[:, :, pl.ds(0, NF)], fw_s.at[1])
+        wait_bytes(rt_out.at[:, :, pl.ds(0, NP)], fw_s.at[1])
         for m in range(2):
             for j in range(NCH):
                 wait_bytes(z_r.at[j, pl.ds(0, NZ - 1 + m)], z_s.at[m, j])
@@ -297,15 +293,13 @@
 
     @pl.when(c == 0)
     def _():
-        wait_bytes(rt_out.at[:, :, pl.ds(0, NF)], fw_r.at[1])
-        wait_bytes(rt_out.at[:, :, pl.ds(0, NP - NF)], dr_r.at[0])
+        wait_bytes(rt_out.at[:, :, pl.ds(0, NP)], fw_r.at[1])
         for j in range(NCH):
             wait_bytes(rs_r.at[0, j], rs_s.at[j])
 
     own = rt_out.at[0, :, 0]
     wait_bytes(own, fw_r.at[0])
     wait_bytes(own, fw_s.at[0])
-    wait_bytes(rt_out.at[0, :, pl.ds(0, NP - NF)], dr_s.at[0])
     wait_bytes(cinv_out.at[oc], co_r.at[0])
     wait_bytes(ot_out.at[oc], co_r.at[1])
     for q in range(NQ):
@@ -409,7 +403,7 @@
             dma((2,)),
             dma((2,)),
         ]
-        + [dma((NCH,)), dma((2, NCH)), dma((2, NCH)), dma((NCH,)), dma((NCH,)), dma((2, NCH, FAR)), dma((2,)), dma((2,)), dma((1,)), dma((1,))]
+        + [dma((NCH,)), dma((2, NCH)), dma((2, NCH)), dma((NCH,)), dma((NCH,)), dma((2, NCH, FAR)), dma((2,)), dma((2,))]
         + [dma((2,)), dma((2,))]
         + [pltpu.SemaphoreType.REGULAR] * 4,
         compiler_params=pltpu.CompilerParams(

time: 36.1 us -> 35.6 us (0.986)
  Pallas kernels: 35.4 us -> 34.9 us
    pallas_call x1, Pallas kernels: 33 us -> 32.6 us  [on_device(): pl.pallas_call(comm_kernel, name='exchange', out_shape=(jax.ShapeDtypeStr...]
where the time goes in v6:
time: 35.6 us; the launch traced here: 35.5 us
  Pallas kernels  34.9 us (98%)
  between operations  0.64 us (2%)
    pallas_call x1, Pallas kernels, on_device(): pl.pallas_call(comm_kernel, name='exchange', out_shape=(jax.ShapeDtypeStr...  32.6 us
    pallas_call x1, Pallas kernels, on_device(): pl.pallas_call(out_kernel, name='decompress', out_shape=(jax.ShapeDtypeSt...  2.33 us

profile of v6, /device:TPU:1, one launch (start us, length us, event | category | flops | bytes accessed | tf_op | source)
XLA Modules:
  0.0 35.5 jit_solution(18011656697076874569)
XLA Ops:
  0.6 32.6 %exchange.1 = (f32[2,2,16,8,256]{4,3,2,1,0:T(8,128)S(1)}, f32[2,64,128]{2,1,0:T(8,128)S(1)}, f32[2,64,256]{2,1,0:T(8,128)S(1)}, f32[2,256,1024]{2,1,0:T(8,128)S(1)}) custom-call(bf16[2,256,1024]{2,1,0:T(8,128)(2,1)} %bitcast.6, f32[2,256,1024]{2,1,0:T(8,128)} %bitcast.5, f32[2,64,1024]{2,1,0:T(8,128)} %bitcast.7), custom_call_target="tpu_custom_call" | custom-call | tf_op jit(solution)/shard_map/exchange/pallas_call | solution.py:366
  33.2 2.3 %decompress.1 = (bf16[2,256,1024]{2,1,0:T(8,128)(2,1)}, f32[2,256,1024]{2,1,0:T(8,128)}, f32[2,64,1024]{2,1,0:T(8,128)}) custom-call(f32[2,256,1024]{2,1,0:T(8,128)S(1)} %get-tuple-element.10.mer_ref, f32[2,2,16,8,256]{4,3,2,1,0:T(8,128)S(1)} %get-tuple-element.11.rt_ref, f32[2,64,128]{2,1,0:T(8,128)S(1)} %get-tuple-element.12.cinv_ref, ...), custom_call_target="tpu_custom_call" | custom-call | tf_op jit(solution)/shard_map/decompress/pallas_call | solution.py:413
